TPU v7x, 512 devices: a whole 4x8x8 slice. The times are simulated.
512 devices in a mesh: xy: 64 (over x, y, core), gz: 8 (over z).
Axes of the slice: x: 4, y: 8, z: 8, core: 2. Of those that a mesh axis runs over, the one named last changes fastest.
Arguments:
- potential_temp: float32 [16, 256, 512], P('gz', 'xy'), may hold values from -6 to 6
- wind_field: float32 [3, 16, 256, 512], P(None, 'gz', 'xy'), may hold values from -0.25 to 0.25
- eddy_diff: float32 [16, 256, 512], P('gz', 'xy'), may hold values from 0.005 to 0.04
- facade_cell: int32 [8, 8192, 128], P('gz', 'xy'), may hold values from 0 to 4095
- tile_send: int32 [8, 8192], P('gz', 'xy'), may hold values from -1 to 127, as said below
- tile_take: int32 [8, 4096], P('gz', 'xy'), may hold values from 0 to 127, as said below
- wall_temp: float32 [8, 4096, 32, 128], P('gz', 'xy'), may hold values from -6 to 6
- wall_class: int32 [8, 4096], P('gz', 'xy'), may hold values from 0 to 3
- wall_inverse: float32 [4, 32, 32], replicated, as said below
- refl_block: bfloat16 [64, 128, 128, 128], P('xy', 'gz'), may hold values from -0.5 to 0.5
- refl_pair: int32 [64, 2, 128], P('xy', None, 'gz'), may hold values from 0 to 511
Outputs:
- temp_next: float32 [16, 256, 512], P('gz', 'xy')
- wall_next: float32 [8, 4096, 32, 128], P('gz', 'xy')
Inputs may be any that keep to these rules, and one draw needn't show every extreme that they name: `tile_send`: in each vertical index, each LES device's live slots carry distinct values dest * 2 + c with c below the number of tiles that it sends to owner dest, and at most 2 tiles go from one LES device to one owner; some LES device has all 128 slots live, with 2 tiles to every owner, and empty slots hold -1. `tile_take`: for owner j at vertical index k, the 64 values are exactly the rows src * 2 + c for which LES device src sends a tile with value j * 2 + c, each once; every owner receives exactly 64 tiles. `wall_inverse`: nonnegative entries, diagonally dominant by rows.
All inputs are finite; a program needn't handle non-finite values.
Results may differ from a plain program's by a relative error of at most 0.0014.
Values may be sent and summed in bfloat16 or wider, within the bound.
No kernel may reach another device: no remote copies, remote signals or barrier semaphores. Data moves between devices by JAX's collectives and lax.ppermute only.
A program may use at most 64 MiB of HBM per device.

v0:
```python
import jax
import jax.numpy as jnp
from jax import lax
from jax.sharding import PartitionSpec as P

SUB = 4


wall_gain = 0.25
flux_gain = 0.5


def with_halo(array, sides, width):
    for axis, dim in sides:
        size, length = (lax.axis_size(axis), array.shape[dim])
        up = [(i, (i + 1) % size) for i in range(size - 1)]
        down = [(j, i) for i, j in up]
        last = lax.slice_in_dim(array, length - width, length, axis=dim)
        initial = lax.slice_in_dim(array, 0, width, axis=dim)
        before = lax.ppermute(last, axis, up)
        after = lax.ppermute(initial, axis, down)
        array = jnp.concatenate([before, array, after], axis=dim)
    return array


def upwind(speed, centre, lower, upper):
    return jnp.maximum(speed, 0.0) * (centre - lower) + jnp.minimum(speed, 0.0) * (upper - centre)


def on_device(
    potential_temp,
    wind_field,
    eddy_diff,
    facade_cell,
    tile_send,
    tile_take,
    wall_temp,
    wall_class,
    wall_inverse,
    refl_block,
    refl_pair,
):
    levels, x_rows, y_cells = potential_temp.shape
    tile_slots = facade_cell.shape[1]
    tile_width = facade_cell.shape[2]
    owned = tile_take.shape[1]
    node_count = wall_temp.shape[2]
    xy_count = lax.axis_size("xy")
    capacity = 2 * owned // xy_count
    slot_total = xy_count * capacity
    speed_sq = (
        wind_field[0] * wind_field[0]
        + wind_field[1] * wind_field[1]
        + wind_field[2] * wind_field[2]
    )
    line_count = levels * x_rows
    both_lines = jnp.concatenate(
        (potential_temp.reshape(line_count, y_cells), speed_sq.reshape(line_count, y_cells)), axis=0
    )
    facade_total = tile_slots * tile_width
    block_size = min(2048, facade_total // 8)
    block_count = facade_total // block_size
    cell_index = facade_cell.reshape(facade_total)
    index_blocks = cell_index.reshape(block_count, block_size)
    lane_ids = lax.broadcasted_iota(jnp.int32, (1, y_cells), 1)
    line_lanes = lax.broadcasted_iota(jnp.int32, (1, line_count), 1)

    def factors(index_block):
        line_hot = ((index_block // y_cells)[:, None] == line_lanes).astype(jnp.float32)
        column_hot = ((index_block % y_cells)[:, None] == lane_ids).astype(jnp.float32)
        return (line_hot, column_hot)

    def lookup(index_block):
        line_hot, column_hot = factors(index_block)
        picked = lax.dot_general(
            column_hot,
            both_lines,
            (((1,), (1,)), ((), ())),
            precision=lax.Precision.HIGHEST,
            preferred_element_type=jnp.float32,
        )
        theta_val = jnp.sum(picked[:, :line_count] * line_hot, axis=1)
        speed_val = jnp.sum(picked[:, line_count:] * line_hot, axis=1)
        return (theta_val, speed_val)

    theta_found, speed_found = lax.map(lookup, index_blocks)
    air_slots = theta_found.reshape(tile_slots, tile_width)
    coef_slots = 0.5 + 4.0 * speed_found.reshape(tile_slots, tile_width)
    send_rows = tile_send.reshape(tile_slots)
    target_rows = jnp.where(send_rows >= 0, send_rows, slot_total)
    empty_box = jnp.zeros((slot_total + 1, tile_width), jnp.float32)
    air_out = empty_box.at[target_rows].set(air_slots)[:slot_total]
    coef_out = empty_box.at[target_rows].set(coef_slots)[:slot_total]
    air_recv, coef_recv = (
        lax.all_to_all(air_out, "xy", split_axis=0, concat_axis=0, tiled=True),
        lax.all_to_all(coef_out, "xy", split_axis=0, concat_axis=0, tiled=True),
    )
    take_rows = tile_take.reshape(owned)
    own_air = air_recv[take_rows]
    own_coef = coef_recv[take_rows]
    wall_state = wall_temp.reshape(owned, node_count, tile_width)
    emitted = wall_state[:, 0, :].astype(jnp.bfloat16)
    district = lax.all_gather(emitted, "gz", axis=0, tiled=True)
    blocks = refl_block[0]
    pair_rows = refl_pair[0]
    source_emit = district[pair_rows[1]]
    contrib = jnp.einsum("bij,bj->bi", blocks, source_emit, preferred_element_type=jnp.float32)
    targets = pair_rows[0]
    district_rows = lax.axis_size("gz") * owned
    row_ids = lax.iota(jnp.int32, district_rows)
    one_hot = (row_ids[:, None] == targets[None, :]).astype(jnp.float32)
    whole = lax.psum(
        jnp.dot(
            one_hot, contrib, precision=lax.Precision.HIGHEST, preferred_element_type=jnp.float32
        ).astype(jnp.bfloat16),
        "gz",
    ).astype(jnp.float32)
    own_rad = lax.dynamic_slice_in_dim(whole, lax.axis_index("gz") * owned, owned, 0)
    class_ids = lax.broadcasted_iota(jnp.int32, (owned, wall_inverse.shape[0]), 1)
    class_hot = (wall_class.reshape(owned)[:, None] == class_ids).astype(jnp.float32)
    inverse_tile = jnp.einsum(
        "tc,cab->tab", class_hot, wall_inverse, precision=lax.Precision.HIGHEST
    )
    temps = wall_state
    for substep in range(SUB):
        forcing = own_coef * (own_air - temps[:, 0, :]) + own_rad
        temps = temps.at[:, 0, :].add(wall_gain * forcing)
        temps = jnp.einsum("tab,tbf->taf", inverse_tile, temps, precision=lax.Precision.HIGHEST)
    flux_out = own_coef * (temps[:, 0, :] - own_air)
    back_rows = jnp.zeros((slot_total, tile_width), jnp.float32).at[take_rows].set(flux_out)
    returned = lax.all_to_all(back_rows, "xy", split_axis=0, concat_axis=0, tiled=True)
    slot_flux = returned[jnp.maximum(send_rows, 0)]
    slot_flux = jnp.where((send_rows >= 0)[:, None], slot_flux, 0.0)
    flux_blocks = slot_flux.reshape(block_count, block_size)

    def deposit(total, inputs):
        index_block, flux_block = inputs
        line_hot, column_hot = factors(index_block)
        weighted = column_hot * flux_block[:, None]
        added = lax.dot_general(
            line_hot,
            weighted,
            (((0,), (0,)), ((), ())),
            precision=lax.Precision.HIGHEST,
            preferred_element_type=jnp.float32,
        )
        return (total + added, None)

    heat_lines, unused = lax.scan(
        deposit, jnp.zeros((line_count, y_cells), jnp.float32), (index_blocks, flux_blocks)
    )
    heat_cells = heat_lines.reshape(levels, x_rows, y_cells)
    padded = with_halo(potential_temp, (("xy", 1), ("gz", 0)), 1)
    lower_z = padded[:-2, 1:-1]
    upper_z = padded[2:, 1:-1]
    lower_x = padded[1:-1, :-2]
    upper_x = padded[1:-1, 2:]
    lower_y = jnp.roll(potential_temp, 1, axis=2)
    upper_y = jnp.roll(potential_temp, -1, axis=2)
    advect = (
        upwind(wind_field[0], potential_temp, lower_z, upper_z)
        + upwind(wind_field[1], potential_temp, lower_x, upper_x)
        + upwind(wind_field[2], potential_temp, lower_y, upper_y)
    )
    laplace = lower_z + upper_z + lower_x + upper_x + lower_y + upper_y - 6.0 * potential_temp
    temp_next = potential_temp - advect + eddy_diff * laplace + flux_gain * heat_cells
    return (temp_next, temps.reshape(1, owned, node_count, tile_width))


def solution(mesh):
    in_specs = (
        P("gz", "xy", None),
        P(None, "gz", "xy", None),
        P("gz", "xy", None),
        P("gz", "xy", None),
        P("gz", "xy"),
        P("gz", "xy"),
        P("gz", "xy", None, None),
        P("gz", "xy"),
        P(),
        P("xy", "gz", None, None),
        P("xy", None, "gz"),
    )
    out_specs = (P("gz", "xy", None), P("gz", "xy", None, None))
    return jax.shard_map(
        on_device, mesh=mesh, in_specs=in_specs, out_specs=out_specs, check_vma=False
    )
```

profile of v0, /device:TPU:1, one launch (start us, length us, event | category | flops | bytes accessed | tf_op | source)
XLA Modules:
  0.0 217.7 jit_solution(7051283349037103455)
XLA Ops:
  9.7 21.8 %while.34 = (s32[]{:T(128)}, f32[8,2048]{1,0:T(8,128)S(1)}, f32[8,2048]{1,0:T(8,128)S(1)}, s32[8,2048]{1,0:T(8,128)S(1)}, f32[16,512]{1,0:T(8,128)S(1)}) while((s32[]{:T(128)}, f32[8,2048]{1,0:T(8,128)S(1)}, f32[8,2048]{1,0:T(8,128)S(1)}, s32[8,2048]{1,0:T(8,128)S(1)}, f32[16,512]{1,0:T(8,128)S(1)}) %tuple.99), condition=%wide.region_3.4_spmd.clone.clone, body=%wide.region_0.3_spmd.clone.sunk.clone | while | flops 202491904 | bytes 401481 | solution.py:86
  9.7 2.2 %fusion.109 = f32[2048,16]{0,1:T(8,128)S(1)} fusion(f32[16,512]{1,0:T(8,128)S(1)} %get-tuple-element.406, s32[2048]{0:T(1024)S(1)} %get-tuple-element.368), kind=kOutput, calls=%fused_computation.12.clone.1.clone | convolution fusion | flops 202375168 | bytes 172032 | tf_op jit(solution)/shard_map/while/body/eval_jaxpr/dot_general | solution.py:75
  12.4 2.2 %fusion.109 = f32[2048,16]{0,1:T(8,128)S(1)} fusion(f32[16,512]{1,0:T(8,128)S(1)} %get-tuple-element.406, s32[2048]{0:T(1024)S(1)} %get-tuple-element.368), kind=kOutput, calls=%fused_computation.12.clone.1.clone | convolution fusion | flops 202375168 | bytes 172032 | tf_op jit(solution)/shard_map/while/body/eval_jaxpr/dot_general | solution.py:75
  15.2 2.2 %fusion.109 = f32[2048,16]{0,1:T(8,128)S(1)} fusion(f32[16,512]{1,0:T(8,128)S(1)} %get-tuple-element.406, s32[2048]{0:T(1024)S(1)} %get-tuple-element.368), kind=kOutput, calls=%fused_computation.12.clone.1.clone | convolution fusion | flops 202375168 | bytes 172032 | tf_op jit(solution)/shard_map/while/body/eval_jaxpr/dot_general | solution.py:75
  17.9 2.2 %fusion.109 = f32[2048,16]{0,1:T(8,128)S(1)} fusion(f32[16,512]{1,0:T(8,128)S(1)} %get-tuple-element.406, s32[2048]{0:T(1024)S(1)} %get-tuple-element.368), kind=kOutput, calls=%fused_computation.12.clone.1.clone | convolution fusion | flops 202375168 | bytes 172032 | tf_op jit(solution)/shard_map/while/body/eval_jaxpr/dot_general | solution.py:75
  20.6 2.2 %fusion.109 = f32[2048,16]{0,1:T(8,128)S(1)} fusion(f32[16,512]{1,0:T(8,128)S(1)} %get-tuple-element.406, s32[2048]{0:T(1024)S(1)} %get-tuple-element.368), kind=kOutput, calls=%fused_computation.12.clone.1.clone | convolution fusion | flops 202375168 | bytes 172032 | tf_op jit(solution)/shard_map/while/body/eval_jaxpr/dot_general | solution.py:75
  23.3 2.2 %fusion.109 = f32[2048,16]{0,1:T(8,128)S(1)} fusion(f32[16,512]{1,0:T(8,128)S(1)} %get-tuple-element.406, s32[2048]{0:T(1024)S(1)} %get-tuple-element.368), kind=kOutput, calls=%fused_computation.12.clone.1.clone | convolution fusion | flops 202375168 | bytes 172032 | tf_op jit(solution)/shard_map/while/body/eval_jaxpr/dot_general | solution.py:75
  26.1 2.2 %fusion.109 = f32[2048,16]{0,1:T(8,128)S(1)} fusion(f32[16,512]{1,0:T(8,128)S(1)} %get-tuple-element.406, s32[2048]{0:T(1024)S(1)} %get-tuple-element.368), kind=kOutput, calls=%fused_computation.12.clone.1.clone | convolution fusion | flops 202375168 | bytes 172032 | tf_op jit(solution)/shard_map/while/body/eval_jaxpr/dot_general | solution.py:75
  28.8 2.2 %fusion.109 = f32[2048,16]{0,1:T(8,128)S(1)} fusion(f32[16,512]{1,0:T(8,128)S(1)} %get-tuple-element.406, s32[2048]{0:T(1024)S(1)} %get-tuple-element.368), kind=kOutput, calls=%fused_computation.12.clone.1.clone | convolution fusion | flops 202375168 | bytes 172032 | tf_op jit(solution)/shard_map/while/body/eval_jaxpr/dot_general | solution.py:75
  33.0 11.6 %all-to-all-start = ((f32[64,2,128]{2,1,0:T(2,128)}), f32[64,2,128]{2,1,0:T(2,128)S(1)}, u32[]{:S(2)}, u32[]{:S(2)}) async-start(f32[64,2,128]{2,1,0:T(2,128)} %bitcast.11), calls=%async_computation | async-start | bytes 131072 | tf_op jit(solution)/shard_map/all_to_all | solution.py:96
  45.4 25.0 %all_gather.3 = bf16[512,128]{1,0:T(8,128)(2,1)S(1)} all-gather(bf16[64,128]{1,0:T(8,128)(2,1)S(1)} %fusion.54), channel_id=1, replica_groups=mesh['xy'=64,'gz'=8] {'gz'}, dimensions={0}, use_global_device_ids=true | all-gather | bytes 147456 | tf_op jit(solution)/shard_map/all_gather | solution.py:103
  72.3 9.6 %collective-permute-start = (f32[2,1,512]{2,1,0:T(1,128)S(1)}, f32[2,1,512]{2,1,0:T(1,128)S(1)}, u32[]{:S(2)}, u32[]{:S(2)}) collective-permute-start(f32[2,1,512]{2,1,0:T(1,128)S(1)} %get-tuple-element.290), channel_id=1, source_target_pairs={{0,8},{8,16},{16,24},{24,32},{32,40},{40,48},{48,56},{56,64},{64,7... | collective-permute-start | bytes 12296 | tf_op jit(solution)/shard_map/ppermute | solution.py:20
  86.2 11.7 %all-to-all-start.1 = ((f32[64,2,128]{2,1,0:T(2,128)}), f32[64,2,128]{2,1,0:T(2,128)S(1)}, u32[]{:S(2)}, u32[]{:S(2)}) async-start(f32[64,2,128]{2,1,0:T(2,128)} %bitcast.17), calls=%async_computation.1 | async-start | bytes 131072 | tf_op jit(solution)/shard_map/all_to_all | solution.py:95
  100.6 7.0 %all-to-all-done.1 = f32[64,2,128]{2,1,0:T(2,128)S(1)} async-done(((f32[64,2,128]{2,1,0:T(2,128)}), f32[64,2,128]{2,1,0:T(2,128)S(1)}, u32[]{:S(2)}, u32[]{:S(2)}) %all-to-all-start.1) | async-done | bytes 65568 | tf_op jit(solution)/shard_map/all_to_all | solution.py:95
  108.3 42.1 %all-reduce.2.cloned.1.call-done = bf16[512,128]{1,0:T(8,128)(2,1)} async-done(((bf16[512,128]{1,0:T(8,128)(2,1)}), bf16[512,128]{1,0:T(8,128)(2,1)}) %all-reduce.2.cloned.1.call-update) | async-done | bytes 131088 | tf_op jit(solution)/shard_map/psum | solution.py:112
  151.7 2.9 %fusion.26 = f32[64,32,128]{2,1,0:T(8,128)S(1)} fusion(f32[64,32,32]{2,1,0:T(8,128)S(1)} %copy.27, f32[64,32,128]{2,0,1:T(8,128)} %fusion.43), kind=kOutput, calls=%fused_computation.49 | convolution fusion | flops 100663296 | bytes 2359296 | tf_op jit(solution)/shard_map/tab,tbf->taf/dot_general | solution.py:128
  160.2 2.4 %fusion.87 = f32[64,32,128]{2,1,0:T(8,128)S(1)} fusion(f32[64,32,32]{2,1,0:T(8,128)S(1)} %copy.27, f32[64,32,128]{2,1,0:T(8,128)} %scatter-add.16), kind=kOutput, calls=%fused_computation.148 | convolution fusion | flops 100663296 | bytes 2359296 | tf_op jit(solution)/shard_map/tab,tbf->taf/dot_general | solution.py:128
  167.2 15.1 %all-to-all-start.2 = ((f32[64,2,128]{2,1,0:T(2,128)}), f32[64,2,128]{2,1,0:T(2,128)S(1)}, u32[]{:S(2)}, u32[]{:S(2)}) async-start(f32[64,2,128]{2,1,0:T(2,128)} %bitcast.38), calls=%async_computation.2 | async-start | bytes 131072 | tf_op jit(solution)/shard_map/all_to_all | solution.py:131
  182.4 2.9 %collective-permute-start.2 = (f32[1,6,512]{2,1,0:T(8,128)S(1)}, f32[1,6,512]{2,1,0:T(8,128)S(1)}, u32[]{:S(2)}, u32[]{:S(2)}) collective-permute-start(f32[1,6,512]{2,1,0:T(8,128)S(1)} %get-tuple-element.284), channel_id=1, source_target_pairs={{0,1},{1,2},{2,3},{3,4},{4,5},{5,6},{6,7},{8,9},{9,10},{10,11},{11... | collective-permute-start | bytes 36872 | tf_op jit(solution)/shard_map/ppermute | solution.py:20
  186.6 5.5 %all-to-all-done.2 = f32[64,2,128]{2,1,0:T(2,128)S(1)} async-done(((f32[64,2,128]{2,1,0:T(2,128)}), f32[64,2,128]{2,1,0:T(2,128)S(1)}, u32[]{:S(2)}, u32[]{:S(2)}) %all-to-all-start.2) | async-done | bytes 65568 | tf_op jit(solution)/shard_map/all_to_all | solution.py:131
  192.9 17.2 %while.35 = (s32[]{:T(128)}, f32[8,512]{1,0:T(8,128)S(1)}, s32[8,2048]{1,0:T(8,128)S(1)}, f32[8,2048]{1,0:T(8,128)S(1)}) while((s32[]{:T(128)}, f32[8,512]{1,0:T(8,128)S(1)}, s32[8,2048]{1,0:T(8,128)S(1)}, f32[8,2048]{1,0:T(8,128)S(1)}) %tuple.107), condition=%wide.region_9.10_spmd.clone.clone, body=%wide.region_8.9_spmd.clone.sunk.clone | while | flops 102823936 | bytes 114759 | solution.py:149
  193.0 2.1 fusion.112
  195.1 2.1 fusion.112
  197.3 2.1 fusion.112
  (163 shorter events, 43.0 us)
Async XLA Ops:
  7.2 63.8 %copy-start = (bf16[1,16,128,128]{3,2,1,0:T(8,128)(2,1)S(1)}, bf16[1,16,128,128]{3,2,1,0:T(8,128)(2,1)}, u32[]{:S(2)}) copy-start(bf16[1,16,128,128]{3,2,1,0:T(8,128)(2,1)} %param.32) | copy-start | bytes 1572868
  9.6 21.9 %copy-start.11 = (s32[1,128]{1,0:T(1,128)S(1)}, s32[1,128]{1,0:T(1,128)}, u32[]{:S(2)}) copy-start(s32[1,128]{1,0:T(1,128)} %param.27) | copy-start | bytes 1540
  9.6 35.1 %copy-start.9 = (s32[1,2,16]{2,1,0:T(2,128)S(1)}, s32[1,2,16]{2,1,0:T(2,128)}, u32[]{:S(2)}) copy-start(s32[1,2,16]{2,1,0:T(2,128)} %param.33) | copy-start | bytes 388
  9.6 35.1 %copy-start.3 = (f32[1,64,32,128]{3,2,1,0:T(8,128)S(1)}, f32[1,64,32,128]{3,2,1,0:T(8,128)}, u32[]{:S(2)}) copy-start(f32[1,64,32,128]{3,2,1,0:T(8,128)} %param.29) | copy-start | bytes 3145732
  33.0 53.2 %all-to-all-start = ((f32[64,2,128]{2,1,0:T(2,128)}), f32[64,2,128]{2,1,0:T(2,128)S(1)}, u32[]{:S(2)}, u32[]{:S(2)}) async-start(f32[64,2,128]{2,1,0:T(2,128)} %bitcast.11), calls=%async_computation | async-start | bytes 131072 | tf_op jit(solution)/shard_map/all_to_all | solution.py:96
  44.6 105.7 %all-reduce.2.cloned.1.call-start = ((), (), s32[]{:S(2)}) async-start(), calls=%async_computation.3 | async-start | bytes 262144 | tf_op jit(solution)/shard_map/psum | solution.py:112
  44.7 27.6 %copy-start.4 = (f32[2,4,512]{2,1,0:T(4,128)S(1)}, f32[2,4,512]{2,1,0:T(4,128)}, u32[]{:S(2)}) copy-start(f32[2,4,512]{2,1,0:T(4,128)} %param.23) | copy-start | bytes 49156
  45.4 38.7 %copy-start.10 = (s32[1,64]{1,0:T(1,128)S(1)}, s32[1,64]{1,0:T(1,128)}, u32[]{:S(2)}) copy-start(s32[1,64]{1,0:T(1,128)} %param.28) | copy-start | bytes 772
  45.4 38.7 %copy-start.6 = (f32[4,32,32]{2,1,0:T(8,128)S(1)}, f32[4,32,32]{2,1,0:T(8,128)}, u32[]{:S(2)}) copy-start(f32[4,32,32]{2,1,0:T(8,128)} %param.31) | copy-start | bytes 49156
  45.4 38.7 %copy-start.8 = (s32[1,64]{1,0:T(1,128)S(1)}, s32[1,64]{1,0:T(1,128)}, u32[]{:S(2)}) copy-start(s32[1,64]{1,0:T(1,128)} %param.30) | copy-start | bytes 772
  72.3 27.7 %collective-permute-start = (f32[2,1,512]{2,1,0:T(1,128)S(1)}, f32[2,1,512]{2,1,0:T(1,128)S(1)}, u32[]{:S(2)}, u32[]{:S(2)}) collective-permute-start(f32[2,1,512]{2,1,0:T(1,128)S(1)} %get-tuple-element.290), channel_id=1, source_target_pairs={{0,8},{8,16},{16,24},{24,32},{32,40},{40,48},{48,56},{56,64},{64,7... | collective-permute-start | bytes 12296 | tf_op jit(solution)/shard_map/ppermute | solution.py:20
  81.9 18.1 %collective-permute-start.1 = (f32[2,1,512]{2,1,0:T(1,128)S(1)}, f32[2,1,512]{2,1,0:T(1,128)S(1)}, u32[]{:S(2)}, u32[]{:S(2)}) collective-permute-start(f32[2,1,512]{2,1,0:T(1,128)S(1)} %get-tuple-element.291), channel_id=1, source_target_pairs={{8,0},{16,8},{24,16},{32,24},{40,32},{48,40},{56,48},{64,56},{72,6... | collective-permute-start | bytes 12296 | tf_op jit(solution)/shard_map/ppermute | solution.py:21
  86.2 21.4 %all-to-all-start.1 = ((f32[64,2,128]{2,1,0:T(2,128)}), f32[64,2,128]{2,1,0:T(2,128)S(1)}, u32[]{:S(2)}, u32[]{:S(2)}) async-start(f32[64,2,128]{2,1,0:T(2,128)} %bitcast.17), calls=%async_computation.1 | async-start | bytes 131072 | tf_op jit(solution)/shard_map/all_to_all | solution.py:95
  156.7 1.0 copy-start.1
  164.9 1.0 copy-start.2
  167.2 24.9 %all-to-all-start.2 = ((f32[64,2,128]{2,1,0:T(2,128)}), f32[64,2,128]{2,1,0:T(2,128)S(1)}, u32[]{:S(2)}, u32[]{:S(2)}) async-start(f32[64,2,128]{2,1,0:T(2,128)} %bitcast.38), calls=%async_computation.2 | async-start | bytes 131072 | tf_op jit(solution)/shard_map/all_to_all | solution.py:131
  182.4 27.7 %collective-permute-start.2 = (f32[1,6,512]{2,1,0:T(8,128)S(1)}, f32[1,6,512]{2,1,0:T(8,128)S(1)}, u32[]{:S(2)}, u32[]{:S(2)}) collective-permute-start(f32[1,6,512]{2,1,0:T(8,128)S(1)} %get-tuple-element.284), channel_id=1, source_target_pairs={{0,1},{1,2},{2,3},{3,4},{4,5},{5,6},{6,7},{8,9},{9,10},{10,11},{11... | collective-permute-start | bytes 36872 | tf_op jit(solution)/shard_map/ppermute | solution.py:20
  185.3 24.8 %collective-permute-start.3 = (f32[1,6,512]{2,1,0:T(8,128)S(1)}, f32[1,6,512]{2,1,0:T(8,128)S(1)}, u32[]{:S(2)}, u32[]{:S(2)}) collective-permute-start(f32[1,6,512]{2,1,0:T(8,128)S(1)} %get-tuple-element.285), channel_id=1, source_target_pairs={{1,0},{2,1},{3,2},{4,3},{5,4},{6,5},{7,6},{9,8},{10,9},{11,10},{12... | collective-permute-start | bytes 36872 | tf_op jit(solution)/shard_map/ppermute | solution.py:21
  192.9 17.2 %copy-start.5 = (f32[3,2,4,512]{3,2,1,0:T(4,128)S(1)}, f32[3,2,4,512]{3,2,1,0:T(4,128)}, u32[]{:S(2)}) copy-start(f32[3,2,4,512]{3,2,1,0:T(4,128)} %param.24) | copy-start | bytes 147460
  192.9 17.2 %copy-start.7 = (f32[2,4,512]{2,1,0:T(4,128)S(1)}, f32[2,4,512]{2,1,0:T(4,128)}, u32[]{:S(2)}) copy-start(f32[2,4,512]{2,1,0:T(4,128)} %param.25) | copy-start | bytes 49156
Sparse Core Ops, SparseCore 0:
  72.4 77.8 all-reduce.1
where the time goes:
time: 219 us; the launch traced here: 218 us
  waiting for transfers between devices  54.7 us (25%)
  starting transfers between devices  54.1 us (25%)
  matrix products  43.6 us (20%)
  blocking collectives  25 us (11%)
  local copies, waits for them, and re-layouts  17.9 us (8%)
  between operations  14.5 us (7%)
  other arithmetic  7.17 us (3%)
    psum x1, waiting for transfers between devices, on_device(): lax.psum(jnp.dot(one_hot, contrib, precision=lax.Precision.HIGHEST, prefe...  42.1 us
    all_gather x1, blocking collectives, on_device(): district = lax.all_gather(emitted, 'gz', axis=0, tiled=True)  25 us
    dot_general x8, matrix products, lookup(): lax.dot_general(column_hot, both_lines, (((1,), (1,)), ((), ())), precisi...  17.5 us
    dot_general x8, matrix products, deposit(): lax.dot_general(line_hot, weighted, (((0,), (0,)), ((), ())), precision=l...  16.6 us
    all_to_all x1, starting transfers between devices, on_device(): lax.all_to_all(back_rows, 'xy', split_axis=0, concat_axis=0, tiled=True)  15.1 us
    ppermute x2, starting transfers between devices, with_halo(): before = lax.ppermute(last, axis, up)  12.5 us
    all_to_all x1, starting transfers between devices, on_device(): lax.all_to_all(air_out, 'xy', split_axis=0, concat_axis=0, tiled=True)  11.7 us
    all_to_all x1, starting transfers between devices, on_device(): lax.all_to_all(coef_out, 'xy', split_axis=0, concat_axis=0, tiled=True)  11.6 us
  transfers between devices with their start and end apart: 8, of which 3 were waited for; matrix products, arithmetic and copies ran while one was open for 12% of the time, Pallas kernels for 0%

commit v1 on v0

v1 whole, which is shorter than its diff:
```python
import functools

import jax
import jax.numpy as jnp
from jax import lax
from jax.experimental import pallas as pl
from jax.experimental.pallas import tpu as pltpu
from jax.sharding import PartitionSpec as P


wall_gain = 0.25
flux_gain = 0.5
FULL = 60 << 20
air_step = 6.0 / 32640.0
coef_step = 0.75 / 32640.0

F32 = jnp.float32
BF16 = jnp.bfloat16
VMEM = pl.BlockSpec(memory_space=pltpu.VMEM)
HBM = pl.BlockSpec(memory_space=pltpu.HBM)
SMEM = pl.BlockSpec(memory_space=pltpu.SMEM)


def sds(shape, dtype):
    return jax.ShapeDtypeStruct(shape, dtype)


def call(body, in_specs, outs, args, scratch=(), flops=0, nbytes=1 << 20, limit=12 << 20):
    return pl.pallas_call(
        body,
        in_specs=in_specs,
        out_specs=tuple(VMEM for _ in outs),
        out_shape=tuple(outs),
        scratch_shapes=list(scratch),
        compiler_params=pltpu.CompilerParams(vmem_limit_bytes=limit),
        cost_estimate=pl.CostEstimate(flops=flops, bytes_accessed=nbytes, transcendentals=0),
    )(*args)


def iota(shape, dim):
    return lax.broadcasted_iota(jnp.int32, shape, dim)


def dot(lhs, rhs, dims=((1,), (0,))):
    return lax.dot_general(lhs, rhs, (dims, ((), ())), preferred_element_type=F32)


def column(row, size):
    picked = jnp.where(iota((size, size), 0) == iota((size, size), 1), row, 0.0)
    return jnp.sum(picked, axis=1, keepdims=True)


def split(value):
    high = value.astype(BF16)
    return high, (value - high.astype(F32)).astype(BF16)


def code(value):
    whole = jnp.round(value)
    high = jnp.floor(whole * (1.0 / 256.0))
    return high.astype(BF16), (whole - 256.0 * high).astype(BF16)


def pack_body(wall_ref, pair_ref, theta_ref, out_ref, node_ref, near_ref, level_ref, ids_ref, plane_ref, sems):
    copies = [
        pltpu.make_async_copy(wall_ref.at[0, :, 0, :], node_ref, sems.at[0]),
        pltpu.make_async_copy(pair_ref, near_ref, sems.at[1]),
        pltpu.make_async_copy(theta_ref, level_ref, sems.at[2]),
    ]
    for copy in copies:
        copy.start()
    level = lax.axis_index("gz")
    parts = out_ref.shape[0]
    owned = node_ref.shape[0]
    ids_ref[...] = jnp.full(ids_ref.shape, -1.0, F32)
    for copy in copies:
        copy.wait()
    target = near_ref[0, 0:1, :]
    blocks = target.shape[1]
    for side in range(2):
        for q in range(4):
            plane_ref[side, 4 * q : 4 * q + 4, :] = level_ref[side, :, 128 * q : 128 * q + 128]
    emitted = node_ref[...].astype(BF16)
    for dest in range(parts):
        near = target - dest * owned
        inside = (near >= 0) & (near < owned)
        ids_ref[0:1, 0:blocks] = jnp.where(inside, near, -1).astype(F32)
        up = jnp.where(level + 1 == dest, plane_ref[1], 0.0)
        down = jnp.where(level - 1 == dest, plane_ref[0], 0.0)
        out_ref[dest, 0:owned, :] = emitted
        out_ref[dest, owned : owned + 16, :] = ids_ref[...].astype(BF16)
        out_ref[dest, owned + 16 : owned + 32, :] = (up + down).astype(BF16)


def lookup_body(theta_ref, wind_ref, cell_ref, send_ref, air_ref, speed_ref, out_ref, theta_tab, speed_tab):
    theta = jnp.concatenate([theta_ref[0], theta_ref[1]], axis=0)
    speed = jnp.zeros_like(theta)
    for d in range(3):
        w = jnp.concatenate([wind_ref[d, 0], wind_ref[d, 1]], axis=0)
        speed = speed + w * w
    for q in range(4):
        theta_tab[8 * q : 8 * q + 8, :] = theta[:, 128 * q : 128 * q + 128]
        speed_tab[8 * q : 8 * q + 8, :] = 4.0 * speed[:, 128 * q : 128 * q + 128]
    slots = cell_ref.shape[0]

    def group(p, carry):
        base = pl.multiple_of(p * 8, 8)
        cells = cell_ref[pl.ds(base, 8), :]
        lane = cells & 127
        line = ((cells >> 7) & 3) * 8 + (cells >> 9)
        air = jnp.zeros((8, 128), F32)
        spd = jnp.zeros((8, 128), F32)
        for r in range(32):
            here = line == r
            for_air = jnp.broadcast_to(theta_tab[r : r + 1, :], (8, 128))
            for_spd = jnp.broadcast_to(speed_tab[r : r + 1, :], (8, 128))
            for_air = jnp.take_along_axis(for_air, lane, axis=1, mode="promise_in_bounds")
            for_spd = jnp.take_along_axis(for_spd, lane, axis=1, mode="promise_in_bounds")
            air = jnp.where(here, for_air, air)
            spd = jnp.where(here, for_spd, spd)
        air_ref[pl.ds(base, 8), :] = air
        speed_ref[pl.ds(base, 8), :] = spd
        return carry

    lax.fori_loop(0, slots // 8, group, 0, unroll=8)
    rows = iota((2 * slots, slots), 0)
    wanted = (rows >> 2) * 2 + (rows & 1)
    is_speed = ((rows >> 1) & 1) == 1
    hit = send_ref[...] == wanted
    pick_air = jnp.where(hit & jnp.logical_not(is_speed), 1.0, 0.0).astype(BF16)
    pick_speed = jnp.where(hit & is_speed, 1.0, 0.0).astype(BF16)
    air_high, air_low = code(air_ref[...] * (1.0 / air_step))
    speed_high, speed_low = code(speed_ref[...] * (1.0 / coef_step))
    out = 256.0 * (dot(pick_air, air_high) + dot(pick_speed, speed_high))
    out = out + (dot(pick_air, air_low) + dot(pick_speed, speed_low))
    out_ref[...] = out.astype(jnp.int32).astype(jnp.int16)


def reflect_body(pair_ref, recv_ref, block_ref, out_ref, add_ref, all_ref, src_ref):
    parts, owned, blocks = recv_ref.shape[0], add_ref.shape[0], block_ref.shape[1]
    lane = iota((1, 128), 1)
    ids = jnp.zeros((1, 128), F32)
    for part in range(parts):
        all_ref[part * owned : (part + 1) * owned, :] = recv_ref[part, 0:owned, :].astype(F32)
        row = recv_ref[part, owned : owned + 16, :].astype(F32)[0:1, :]
        row = jnp.where(lane < blocks, row, 0.0)
        ids = ids + (pltpu.roll(row, part * blocks, 1) if part else row)
    for b in range(blocks):
        src_ref[b : b + 1, :] = all_ref[pl.ds(pair_ref[0, 1, b], 1), :]
    source = src_ref[...].astype(BF16)
    which = iota((blocks, 128), 0)
    total = jnp.zeros((blocks, 128), F32)
    for b in range(blocks):
        one = dot(source, block_ref[0, b], ((1,), (1,)))
        total = jnp.where(which == b, one, total)
    for part in range(parts):
        out_ref[part] = total.astype(BF16)
    hot = iota(add_ref.shape, 0).astype(F32) == ids
    add_ref[...] = jnp.where(hot, 1.0, 0.0).astype(BF16)


def wall_body(
    class_ref, inverse_ref, wall_ref, take_ref, free_ref, rows_ref, gain_ref, resp_ref, take_out, back_out, lhs_ref,
):
    nodes = inverse_ref.shape[1]
    full = functools.partial(
        lax.dot_general,
        dimension_numbers=(((1,), (0,)), ((), ())),
        precision=lax.Precision.HIGHEST,
        preferred_element_type=F32,
    )
    for c in range(inverse_ref.shape[0]):
        one = inverse_ref[c]
        two = full(one, one)
        three = full(two, one)
        four = full(two, two)
        stack = jnp.concatenate(
            [four, one[0:1], two[0:1], three[0:1], jnp.zeros((13, nodes), F32)], axis=0
        )
        high, low = split(stack)
        lhs_ref[c] = jnp.concatenate([high, high, low], axis=1)
        for k, power in enumerate((one, two, three, four)):
            resp_ref[c, k] = jnp.broadcast_to(power[:, 0:1], (nodes, 128))

    owned = wall_ref.shape[1]

    def tiles(g, carry):
        base = pl.multiple_of(g * 8, 8)
        firsts = [[], [], [], [], []]
        gains = [[], [], [], []]
        for q in range(8):
            t = base + q
            kind = class_ref[0, t]
            state = wall_ref[0, t]
            high, low = split(state)
            result = dot(lhs_ref[kind], jnp.concatenate([high, low, high], axis=0))
            free_ref[t] = result[0:nodes]
            for k in range(3):
                firsts[k].append(result[nodes + k : nodes + k + 1])
            firsts[3].append(state[0:1])
            firsts[4].append(result[0:1])
            for k in range(4):
                gains[k].append(resp_ref[kind, k, 0:1, :])
        for k in range(5):
            rows_ref[k, pl.ds(base, 8), :] = jnp.concatenate(firsts[k], axis=0)
        for k in range(4):
            gain_ref[k, pl.ds(base, 8), :] = jnp.concatenate(gains[k], axis=0)
        return carry

    lax.fori_loop(0, owned // 8, tiles, 0, unroll=2)
    take = take_ref[...]
    col = column(take.astype(F32), owned).astype(jnp.int32)
    place = (col >> 1) * 4 + (col & 1)
    lanes = iota((owned, take_out.shape[1]), 1)
    take_out[0:owned, :] = jnp.where(lanes == place, 1.0, 0.0).astype(BF16)
    take_out[owned : 2 * owned, :] = jnp.where(lanes == place + 2, 1.0, 0.0).astype(BF16)
    back_out[...] = jnp.where(iota((2 * owned, owned), 0) == take, 1.0, 0.0).astype(BF16)


def force_body(recv_ref, take_ref, back_ref, refl_ref, add_ref, rows_ref, gain_ref, force_ref, out_ref):
    owned = add_ref.shape[0]
    high, low = code(recv_ref[...].astype(jnp.int32).astype(F32))
    both = 256.0 * dot(take_ref[...], high) + dot(take_ref[...], low)
    air = air_step * both[0:owned]
    coef = 0.5 + coef_step * both[owned : 2 * owned]
    parts, blocks = refl_ref.shape[0], refl_ref.shape[1]
    rad = dot(add_ref[...], refl_ref[...].reshape(parts * blocks, 128))
    g1, g2, g3, g4 = gain_ref[0], gain_ref[1], gain_ref[2], gain_ref[3]
    f0 = wall_gain * (coef * (air - rows_ref[3]) + rad)
    f1 = wall_gain * (coef * (air - (rows_ref[0] + g1 * f0)) + rad)
    f2 = wall_gain * (coef * (air - (rows_ref[1] + (g2 * f0 + g1 * f1))) + rad)
    f3 = wall_gain * (coef * (air - (rows_ref[2] + (g3 * f0 + g2 * f1 + g1 * f2))) + rad)
    force_ref[0] = f0
    force_ref[1] = f1
    force_ref[2] = f2
    force_ref[3] = f3
    surface = rows_ref[4] + (g4 * f0 + g3 * f1 + g2 * f2 + g1 * f3)
    high, low = split(surface)
    out_ref[...] = dot(back_ref[...], high) + dot(back_ref[...], low)


def upwind(speed, centre, lower, upper):
    return jnp.maximum(speed, 0.0) * (centre - lower) + jnp.minimum(speed, 0.0) * (upper - centre)


def finish_body(
    class_ref, free_ref, force_ref, resp_ref, send_ref, speed_ref, theta_ref, wind_ref, eddy_ref, zhalo_ref,
    before_ref, after_ref, out_ref, pick_ref, coef_ref, base_ref,
):
    def tile(t, carry):
        kind = class_ref[0, t]
        value = free_ref[t]
        for k in range(4):
            value = value + resp_ref[kind, 3 - k] * force_ref[k, pl.ds(t, 1), :]
        out_ref[0, t] = value
        return carry

    lax.fori_loop(0, free_ref.shape[0], tile, 0, unroll=4)
    slots = send_ref.shape[1]
    slot_col = column(send_ref[...].astype(F32), slots)
    pick_ref[...] = jnp.where(iota((slots, slots), 1).astype(F32) == slot_col, 1.0, 0.0).astype(BF16)
    coef_ref[...] = jnp.where(slot_col >= 0.0, 0.5 + speed_ref[...], 0.0)
    level = lax.axis_index("gz")
    parts = zhalo_ref.shape[0]

    def plane(from_part, valid):
        value = zhalo_ref[jnp.clip(from_part, 0, parts - 1)].astype(F32)
        value = jnp.concatenate([value[4 * q : 4 * q + 4] for q in range(4)], axis=1)
        return jnp.where(valid, value, 0.0)

    below = plane(level - 1, level > 0)
    above = plane(level + 1, level < parts - 1)
    for k in range(2):
        c = theta_ref[k]
        lower_z = theta_ref[0] if k else below
        upper_z = above if k else theta_ref[1]
        lower_x = jnp.concatenate([before_ref[k], c[0:3]], axis=0)
        upper_x = jnp.concatenate([c[1:4], after_ref[k]], axis=0)
        lower_y = jnp.concatenate([c[:, -1:], c[:, :-1]], axis=1)
        upper_y = jnp.concatenate([c[:, 1:], c[:, :1]], axis=1)
        advect = (
            upwind(wind_ref[0, k], c, lower_z, upper_z)
            + upwind(wind_ref[1, k], c, lower_x, upper_x)
            + upwind(wind_ref[2, k], c, lower_y, upper_y)
        )
        laplace = lower_z + upper_z + lower_x + upper_x + lower_y + upper_y - 6.0 * c
        base_ref[k] = c - advect + eddy_ref[k] * laplace


def deposit_body(recv_ref, pick_ref, air_ref, coef_ref, cell_ref, base_ref, out_ref, flux_ref, acc_ref):
    slots = cell_ref.shape[0]
    high, low = split(recv_ref[...])
    surface = dot(pick_ref[...], high) + dot(pick_ref[...], low)
    flux_ref[...] = coef_ref[...] * (surface - air_ref[...])
    count = 8
    lanes = iota((128, count * 128), 0).astype(BF16)
    lines = iota((32, count * 128), 0).astype(BF16)
    acc_ref[...] = jnp.zeros_like(acc_ref)

    def flat(rows):
        return jnp.concatenate([rows[i : i + 1] for i in range(count)], axis=1)

    def group(p, carry):
        base = pl.multiple_of(p * count, count)
        cells = cell_ref[pl.ds(base, count), :]
        lane = flat((cells & 127).astype(F32)).astype(BF16)
        line = flat((((cells >> 7) & 3) * 8 + (cells >> 9)).astype(F32)).astype(BF16)
        high, low = split(flat(flux_ref[pl.ds(base, count), :]))
        hot = jnp.where(lanes == lane, BF16(1), BF16(0))
        here = lines == line
        placed = jnp.concatenate([jnp.where(here, high, BF16(0)), jnp.where(here, low, BF16(0))], axis=0)
        acc_ref[...] += dot(hot, placed, ((1,), (1,)))
        return carry

    lax.fori_loop(0, slots // count, group, 0, unroll=8)
    heat = acc_ref[...].T
    heat = heat[0:32] + heat[32:64]
    heat = jnp.concatenate([heat[8 * q : 8 * q + 8] for q in range(4)], axis=1)
    for k in range(2):
        out_ref[k] = base_ref[k] + flux_gain * heat[4 * k : 4 * k + 4]


def on_device(
    potential_temp,
    wind_field,
    eddy_diff,
    facade_cell,
    tile_send,
    tile_take,
    wall_temp,
    wall_class,
    wall_inverse,
    refl_block,
    refl_pair,
):
    slots = facade_cell.shape[1]
    owned = tile_take.shape[1]
    nodes = wall_temp.shape[2]
    classes = wall_inverse.shape[0]
    blocks = refl_block.shape[1]
    parts = lax.axis_size("gz")
    xy_count = lax.axis_size("xy")
    cells = facade_cell.reshape(slots, 128)
    dma = pltpu.SemaphoreType.DMA

    (payload,) = call(
        pack_body,
        [HBM] * 3,
        [sds((parts, owned + 32, 128), BF16)],
        (wall_temp, refl_pair, potential_temp),
        [
            pltpu.VMEM((owned, 128), F32),
            pltpu.VMEM(refl_pair.shape, jnp.int32),
            pltpu.VMEM(potential_temp.shape, F32),
            pltpu.VMEM((16, 128), F32),
            pltpu.VMEM((2, 16, 128), F32),
            dma((3,)),
        ],
        limit=FULL,
    )
    district = lax.all_to_all(payload, "gz", split_axis=0, concat_axis=0, tiled=True)

    air, speed, send_list = call(
        lookup_body,
        [VMEM] * 4,
        [sds((slots, 128), F32), sds((slots, 128), F32), sds((2 * slots, 128), jnp.int16)],
        (potential_temp, wind_field, cells, tile_send),
        [pltpu.VMEM((32, 128), F32), pltpu.VMEM((32, 128), F32)],
        flops=2 * 48 * 256 * slots * 128,
    )
    free, rows, gain, resp, take_pick, back_pick = call(
        wall_body,
        [SMEM] + [VMEM] * 3,
        [
            sds((owned, nodes, 128), F32),
            sds((5, owned, 128), F32),
            sds((4, owned, 128), F32),
            sds((classes, 4, nodes, 128), F32),
            sds((2 * owned, 2 * slots), BF16),
            sds((2 * owned, owned), BF16),
        ],
        (wall_class, wall_inverse, wall_temp, tile_take),
        [pltpu.VMEM((classes, nodes + 16, 3 * nodes), BF16)],
        flops=2 * 48 * 96 * owned * 128,
    )
    send_list, district, rows = lax.optimization_barrier((send_list, district, rows))
    received = lax.all_to_all(send_list, "xy", split_axis=0, concat_axis=0, tiled=True)

    last = xy_count - 1
    before = lax.ppermute(potential_temp[:, 3:4, :], "xy", [(i, i + 1) for i in range(last)])
    after = lax.ppermute(potential_temp[:, 0:1, :], "xy", [(i + 1, i) for i in range(last)])

    contrib, add_matrix = call(
        reflect_body,
        [SMEM, VMEM, VMEM],
        [sds((parts, blocks, 128), BF16), sds((owned, 128), BF16)],
        (refl_pair, district, refl_block),
        [pltpu.VMEM((parts * owned, 128), F32), pltpu.VMEM((blocks, 128), F32)],
    )
    contrib, received = lax.optimization_barrier((contrib, received))
    reflected = lax.all_to_all(contrib, "gz", split_axis=0, concat_axis=0, tiled=True)

    force, back_list = call(
        force_body,
        [VMEM] * 7,
        [sds((4, owned, 128), F32), sds((2 * owned, 128), F32)],
        (received, take_pick, back_pick, reflected, add_matrix, rows, gain),
    )
    returned = lax.all_to_all(back_list, "xy", split_axis=0, concat_axis=0, tiled=True)
    wall_next, pick, coef, base = call(
        finish_body,
        [SMEM] + [VMEM] * 11,
        [
            sds((1, owned, nodes, 128), F32),
            sds((slots, slots), BF16),
            sds((slots, 128), F32),
            sds(potential_temp.shape, F32),
        ],
        (
            wall_class, free, force, resp, tile_send, speed, potential_temp, wind_field, eddy_diff,
            district[:, owned + 16 : owned + 32, :], before, after,
        ),
    )
    (temp_next,) = call(
        deposit_body,
        [VMEM] * 6,
        [sds(potential_temp.shape, F32)],
        (returned, pick, air, coef, cells, base),
        [pltpu.VMEM((slots, 128), F32), pltpu.VMEM((128, 64), F32)],
        flops=2 * 64 * 128 * slots * 128,
    )
    return temp_next, wall_next


def solution(mesh):
    in_specs = (
        P("gz", "xy", None),
        P(None, "gz", "xy", None),
        P("gz", "xy", None),
        P("gz", "xy", None),
        P("gz", "xy"),
        P("gz", "xy"),
        P("gz", "xy", None, None),
        P("gz", "xy"),
        P(),
        P("xy", "gz", None, None),
        P("xy", None, "gz"),
    )
    out_specs = (P("gz", "xy", None), P("gz", "xy", None, None))
    return jax.shard_map(
        on_device, mesh=mesh, in_specs=in_specs, out_specs=out_specs, check_vma=False
    )
```

time: 219 us -> 76.2 us (0.35)
  the two profiles are of different devices: /device:TPU:1 before, /device:TPU:6 now
where the time goes in v1:
time: 76.2 us; the launch traced here: 75.7 us
  starting transfers between devices  34.4 us (45%)
  waiting for transfers between devices  16.9 us (22%)
  Pallas kernels  12.5 us (16%)
  blocking collectives  10.4 us (14%)
  between operations  0.85 us (1%)
    pallas_call x7, Pallas kernels, call(): pl.pallas_call(body, in_specs=in_specs, out_specs=tuple((VMEM for _ in ou...  12.5 us
    all_to_all x1, starting transfers between devices, on_device(): lax.all_to_all(send_list, 'xy', split_axis=0, concat_axis=0, tiled=True)  10.9 us
    all_to_all x1, starting transfers between devices, on_device(): lax.all_to_all(payload, 'gz', split_axis=0, concat_axis=0, tiled=True)  10.5 us
    all_to_all x1, blocking collectives, on_device(): lax.all_to_all(contrib, 'gz', split_axis=0, concat_axis=0, tiled=True)  10.4 us
    all_to_all x1, waiting for transfers between devices, on_device(): lax.all_to_all(send_list, 'xy', split_axis=0, concat_axis=0, tiled=True)  6.87 us
    all_to_all x1, starting transfers between devices, on_device(): lax.all_to_all(back_list, 'xy', split_axis=0, concat_axis=0, tiled=True)  6.51 us
    ppermute x1, waiting for transfers between devices, on_device(): lax.ppermute(potential_temp[:, 3:4, :], 'xy', [(i, i + 1) for i in range(...  5.07 us
    all_to_all x1, waiting for transfers between devices, on_device(): lax.all_to_all(payload, 'gz', split_axis=0, concat_axis=0, tiled=True)  4.92 us
  transfers between devices with their start and end apart: 5, of which 3 were waited for; matrix products, arithmetic and copies ran while one was open for 0% of the time, Pallas kernels for 10%

profile of v1, /device:TPU:6, one launch (start us, length us, event | category | flops | bytes accessed | tf_op | source)
XLA Modules:
  0.0 75.7 jit_solution(9334155923708079248)
XLA Ops:
  0.6 1.6 %shard_map.123 = bf16[8,96,128]{2,1,0:T(8,128)(2,1)} custom-call(f32[1,64,32,128]{3,2,1,0:T(8,128)} %wall_ref.3, s32[1,2,16]{2,1,0:T(2,128)} %pair_ref.3, f32[2,4,512]{2,1,0:T(4,128)} %theta_ref.5), custom_call_target="tpu_custom_call" | custom-call | bytes 1048576 | tf_op jit(solution)/shard_map/pallas_call | solution.py:29
  2.3 0.0 copy-start.3
  2.3 0.0 copy-start.7
  2.3 0.0 copy-start.8
  2.3 10.5 %all-to-all-start = ((bf16[8,96,128]{2,1,0:T(8,128)(2,1)}), bf16[8,96,128]{2,1,0:T(8,128)(2,1)S(1)}, u32[]{:S(2)}, u32[]{:S(2)}) async-start(bf16[8,96,128]{2,1,0:T(8,128)(2,1)} %shard_map.123), calls=%async_computation | async-start | bytes 393216 | tf_op jit(solution)/shard_map/all_to_all | solution.py:361
  12.8 0.0 copy-start.2
  12.8 0.0 copy-start.4
  12.8 0.0 copy-start.10
  12.8 2.7 %shard_map.124 = (f32[64,32,128]{2,1,0:T(8,128)S(1)}, f32[5,64,128]{2,1,0:T(8,128)S(1)}, f32[4,64,128]{2,1,0:T(8,128)S(1)}, f32[4,4,32,128]{3,2,1,0:T(8,128)S(1)...) custom-call(s32[1,64]{1,0:T(1,128)S(1)} %copy-done.7, f32[4,32,32]{2,1,0:T(8,128)S(1)} %copy-done.3, ...), custom_call_target="tpu_custom_call" | custom-call | flops 75497472 | bytes 1048576 | tf_op jit(solution)/shard_map/pallas_call | solution.py:29
  15.5 0.0 copy-start.9
  15.5 0.6 copy-done.9
  16.2 2.1 %shard_map.122 = (f32[128,128]{1,0:T(8,128)S(1)}, f32[128,128]{1,0:T(8,128)S(1)}, s16[256,128]{1,0:T(8,128)(2,1)}) custom-call(f32[2,4,512]{2,1,0:T(4,128)S(1)} %copy-done.2, f32[3,2,4,512]{3,2,1,0:T(4,128)S(1)} %copy-done.4, s32[128,128]{1,0:T(8,128)S(1)} %bitcast.7, s32[1,128]{1,0:T(1,128)S(1)} %copy-done.9), custom_call_target="tpu_custom_call" | custom-call | flops 402653184 | bytes 1048576 | tf_op jit(solution)/shard_map/pallas_call | solution.py:29
  18.3 4.9 %all-to-all-done.recv_ref = bf16[8,96,128]{2,1,0:T(8,128)(2,1)S(1)} async-done(((bf16[8,96,128]{2,1,0:T(8,128)(2,1)}), bf16[8,96,128]{2,1,0:T(8,128)(2,1)S(1)}, u32[]{:S(2)}, u32[]{:S(2)}) %all-to-all-start) | async-done | bytes 196640 | tf_op jit(solution)/shard_map/all_to_all | solution.py:361
  23.2 10.9 %all-to-all-start.1 = ((s16[64,4,128]{2,1,0:T(4,128)(2,1)}), s16[64,4,128]{2,1,0:T(4,128)(2,1)S(1)}, u32[]{:S(2)}, u32[]{:S(2)}) async-start(s16[64,4,128]{2,1,0:T(4,128)(2,1)} %bitcast.1), calls=%async_computation.1 | async-start | bytes 131072 | tf_op jit(solution)/shard_map/all_to_all | solution.py:387
  34.2 0.9 %shard_map.125 = (bf16[8,16,128]{2,1,0:T(8,128)(2,1)S(1)}, bf16[64,128]{1,0:T(8,128)(2,1)S(1)}) custom-call(s32[1,2,16]{2,1,0:T(2,128)S(1)} %copy-done.6, bf16[8,96,128]{2,1,0:T(8,128)(2,1)S(1)} %all-to-all-done.recv_ref, bf16[1,16,128,128]{3,2,1,0:T(8,128)(2,1)S(1)} %copy-done.1), custom_call_target="tpu_custom_call" | custom-call | bytes 1048576 | tf_op jit(solution)/shard_map/pallas_call | solution.py:29
  35.1 6.9 %all-to-all-done.1 = s16[64,4,128]{2,1,0:T(4,128)(2,1)S(1)} async-done(((s16[64,4,128]{2,1,0:T(4,128)(2,1)}), s16[64,4,128]{2,1,0:T(4,128)(2,1)S(1)}, u32[]{:S(2)}, u32[]{:S(2)}) %all-to-all-start.1) | async-done | bytes 65568 | tf_op jit(solution)/shard_map/all_to_all | solution.py:387
  41.9 10.4 %all_to_all.33.refl_ref = bf16[8,16,128]{2,1,0:T(8,128)(2,1)S(1)} all-to-all(bf16[8,16,128]{2,1,0:T(8,128)(2,1)S(1)} %get-tuple-element.32), channel_id=1, replica_groups=mesh['xy'=64,'gz'=8] {'gz'}, dimensions={0} | all-to-all | bytes 65536 | tf_op jit(solution)/shard_map/all_to_all | solution.py:401
  52.3 1.0 %shard_map.126 = (f32[4,64,128]{2,1,0:T(8,128)S(1)}, f32[128,128]{1,0:T(8,128)}) custom-call(s16[256,128]{1,0:T(8,128)(2,1)S(1)} %bitcast.5, bf16[128,256]{1,0:T(8,128)(2,1)S(1)} %get-tuple-element.30.take_ref, bf16[128,64]{1,0:T(8,128)(2,1)S(1)} %get-tuple-element.31.back_ref, bf16[8,16,128]{2,1,0:T(8,128)(2,1)S(1)} %all_to_all.33.refl_ref, ...), custom_call_target="tpu_custom_call" | custom-call | bytes 1048576 | tf_op jit(solution)/shard_map/pallas_call | solution.py:29
  53.4 6.5 %all-to-all-start.3 = ((f32[64,2,128]{2,1,0:T(2,128)}), f32[64,2,128]{2,1,0:T(2,128)S(1)}, u32[]{:S(2)}, u32[]{:S(2)}) async-start(f32[64,2,128]{2,1,0:T(2,128)} %bitcast.3), calls=%async_computation.3 | async-start | bytes 131072 | tf_op jit(solution)/shard_map/all_to_all | solution.py:409
  59.9 4.6 %collective-permute-start.1 = (f32[2,1,512]{2,1,0:T(1,128)S(1)}, f32[2,1,512]{2,1,0:T(1,128)S(1)}, u32[]{:S(2)}, u32[]{:S(2)}) collective-permute-start(f32[2,1,512]{2,1,0:T(1,128)S(1)} %get-tuple-element.46), channel_id=1, source_target_pairs={{8,0},{16,8},{24,16},{32,24},{40,32},{48,40},{56,48},{64,56},{72,6... | collective-permute-start | bytes 12296 | tf_op jit(solution)/shard_map/ppermute | solution.py:391
  64.5 1.9 %collective-permute-start = (f32[2,1,512]{2,1,0:T(1,128)S(1)}, f32[2,1,512]{2,1,0:T(1,128)S(1)}, u32[]{:S(2)}, u32[]{:S(2)}) collective-permute-start(f32[2,1,512]{2,1,0:T(1,128)S(1)} %get-tuple-element.47), channel_id=1, source_target_pairs={{0,8},{8,16},{16,24},{24,32},{32,40},{40,48},{48,56},{56,64},{64,7... | collective-permute-start | bytes 12296 | tf_op jit(solution)/shard_map/ppermute | solution.py:390
  66.4 5.1 %collective-permute-done.before_ref = f32[2,1,512]{2,1,0:T(1,128)S(1)} collective-permute-done((f32[2,1,512]{2,1,0:T(1,128)S(1)}, f32[2,1,512]{2,1,0:T(1,128)S(1)}, u32[]{:S(2)}, u32[]{:S(2)}) %collective-permute-start) | collective-permute-done | bytes 4128 | tf_op jit(solution)/shard_map/ppermute | solution.py:390
  71.5 1.9 %shard_map.127 = (f32[1,64,32,128]{3,2,1,0:T(8,128)}, bf16[128,128]{1,0:T(8,128)(2,1)S(1)}, f32[128,128]{1,0:T(8,128)S(1)}, f32[2,4,512]{2,1,0:T(4,128)S(1)}) custom-call(s32[1,64]{1,0:T(1,128)S(1)} %copy-done.7, f32[64,32,128]{2,1,0:T(8,128)S(1)} %get-tuple-element.37.free_ref, f32[4,64,128]{2,1,0:T(8,128)S(1)} %get-tuple-element.38.force_ref, ...), custom_call_target="tpu_custom_call" | custom-call | bytes 1048576 | tf_op jit(solution)/shard_map/pallas_call | solution.py:29
  73.5 2.3 %shard_map.128 = f32[2,4,512]{2,1,0:T(4,128)} custom-call(f32[128,128]{1,0:T(8,128)S(1)} %bitcast.6, bf16[128,128]{1,0:T(8,128)(2,1)S(1)} %get-tuple-element.41.pick_ref, f32[128,128]{1,0:T(8,128)S(1)} %get-tuple-element.42.air_ref, f32[128,128]{1,0:T(8,128)S(1)} %get-tuple-element.43.coef_ref, s32[128,128]{1,0:T(8,128)S(1)} %bitcast.8, ...), custom_call_target="tpu_custom_call" | custom-call | flops 268435456 | bytes 1048576 | tf_op jit(solution)/shard_map/pallas_call | solution.py:29
  (18 shorter events, 0.0 us)
Async XLA Ops:
  0.6 12.1 %copy-start = (f32[1,64,32,128]{3,2,1,0:T(8,128)S(1)}, f32[1,64,32,128]{3,2,1,0:T(8,128)}, u32[]{:S(2)}) copy-start(f32[1,64,32,128]{3,2,1,0:T(8,128)} %wall_ref.3) | copy-start | bytes 3145732
  2.3 10.5 %copy-start.3 = (f32[4,32,32]{2,1,0:T(8,128)S(1)}, f32[4,32,32]{2,1,0:T(8,128)}, u32[]{:S(2)}) copy-start(f32[4,32,32]{2,1,0:T(8,128)} %inverse_ref.1) | copy-start | bytes 49156
  2.3 10.5 %copy-start.7 = (s32[1,64]{1,0:T(1,128)S(1)}, s32[1,64]{1,0:T(1,128)}, u32[]{:S(2)}) copy-start(s32[1,64]{1,0:T(1,128)} %class_ref.3) | copy-start | bytes 772
  2.3 10.5 %copy-start.8 = (s32[1,64]{1,0:T(1,128)S(1)}, s32[1,64]{1,0:T(1,128)}, u32[]{:S(2)}) copy-start(s32[1,64]{1,0:T(1,128)} %take_ref.1) | copy-start | bytes 772
  2.3 20.9 %all-to-all-start = ((bf16[8,96,128]{2,1,0:T(8,128)(2,1)}), bf16[8,96,128]{2,1,0:T(8,128)(2,1)S(1)}, u32[]{:S(2)}, u32[]{:S(2)}) async-start(bf16[8,96,128]{2,1,0:T(8,128)(2,1)} %shard_map.123), calls=%async_computation | async-start | bytes 393216 | tf_op jit(solution)/shard_map/all_to_all | solution.py:361
  12.8 2.7 %copy-start.2 = (f32[2,4,512]{2,1,0:T(4,128)S(1)}, f32[2,4,512]{2,1,0:T(4,128)}, u32[]{:S(2)}) copy-start(f32[2,4,512]{2,1,0:T(4,128)} %theta_ref.5) | copy-start | bytes 49156
  12.8 2.7 %copy-start.4 = (f32[3,2,4,512]{3,2,1,0:T(4,128)S(1)}, f32[3,2,4,512]{3,2,1,0:T(4,128)}, u32[]{:S(2)}) copy-start(f32[3,2,4,512]{3,2,1,0:T(4,128)} %wind_ref.3) | copy-start | bytes 147460
  12.8 2.7 %copy-start.10 = (s32[1,128,128]{2,1,0:T(8,128)S(1)}, s32[1,128,128]{2,1,0:T(8,128)}, u32[]{:S(2)}) copy-start(s32[1,128,128]{2,1,0:T(8,128)} %param.14) | copy-start | bytes 196612
  15.5 0.7 copy-start.9
  16.2 18.0 %copy-start.1 = (bf16[1,16,128,128]{3,2,1,0:T(8,128)(2,1)S(1)}, bf16[1,16,128,128]{3,2,1,0:T(8,128)(2,1)}, u32[]{:S(2)}) copy-start(bf16[1,16,128,128]{3,2,1,0:T(8,128)(2,1)} %block_ref.1) | copy-start | bytes 1572868
  23.2 11.0 %copy-start.6 = (s32[1,2,16]{2,1,0:T(2,128)S(1)}, s32[1,2,16]{2,1,0:T(2,128)}, u32[]{:S(2)}) copy-start(s32[1,2,16]{2,1,0:T(2,128)} %pair_ref.3) | copy-start | bytes 388
  23.2 18.7 %all-to-all-start.1 = ((s16[64,4,128]{2,1,0:T(4,128)(2,1)}), s16[64,4,128]{2,1,0:T(4,128)(2,1)S(1)}, u32[]{:S(2)}, u32[]{:S(2)}) async-start(s16[64,4,128]{2,1,0:T(4,128)(2,1)} %bitcast.1), calls=%async_computation.1 | async-start | bytes 131072 | tf_op jit(solution)/shard_map/all_to_all | solution.py:387
  53.4 20.1 %all-to-all-start.3 = ((f32[64,2,128]{2,1,0:T(2,128)}), f32[64,2,128]{2,1,0:T(2,128)S(1)}, u32[]{:S(2)}, u32[]{:S(2)}) async-start(f32[64,2,128]{2,1,0:T(2,128)} %bitcast.3), calls=%async_computation.3 | async-start | bytes 131072 | tf_op jit(solution)/shard_map/all_to_all | solution.py:409
  59.9 6.6 %collective-permute-start.1 = (f32[2,1,512]{2,1,0:T(1,128)S(1)}, f32[2,1,512]{2,1,0:T(1,128)S(1)}, u32[]{:S(2)}, u32[]{:S(2)}) collective-permute-start(f32[2,1,512]{2,1,0:T(1,128)S(1)} %get-tuple-element.46), channel_id=1, source_target_pairs={{8,0},{16,8},{24,16},{32,24},{40,32},{48,40},{56,48},{64,56},{72,6... | collective-permute-start | bytes 12296 | tf_op jit(solution)/shard_map/ppermute | solution.py:391
  64.5 7.0 %collective-permute-start = (f32[2,1,512]{2,1,0:T(1,128)S(1)}, f32[2,1,512]{2,1,0:T(1,128)S(1)}, u32[]{:S(2)}, u32[]{:S(2)}) collective-permute-start(f32[2,1,512]{2,1,0:T(1,128)S(1)} %get-tuple-element.47), channel_id=1, source_target_pairs={{0,8},{8,16},{16,24},{24,32},{32,40},{40,48},{48,56},{56,64},{64,7... | collective-permute-start | bytes 12296 | tf_op jit(solution)/shard_map/ppermute | solution.py:390
  66.4 5.1 %copy-start.5 = (f32[2,4,512]{2,1,0:T(4,128)S(1)}, f32[2,4,512]{2,1,0:T(4,128)}, u32[]{:S(2)}) copy-start(f32[2,4,512]{2,1,0:T(4,128)} %eddy_ref.1) | copy-start | bytes 49156

commit v2 on v1

--- a/solution.py
+++ b/solution.py
@@ -11,8 +11,6 @@
 wall_gain = 0.25
 flux_gain = 0.5
 FULL = 60 << 20
-air_step = 6.0 / 32640.0
-coef_step = 0.75 / 32640.0
 
 F32 = jnp.float32
 BF16 = jnp.bfloat16
@@ -25,11 +23,11 @@
     return jax.ShapeDtypeStruct(shape, dtype)
 
 
-def call(body, in_specs, outs, args, scratch=(), flops=0, nbytes=1 << 20, limit=12 << 20):
+def call(body, in_specs, outs, args, scratch=(), flops=0, nbytes=1 << 20, limit=12 << 20, out_specs=None):
     return pl.pallas_call(
         body,
         in_specs=in_specs,
-        out_specs=tuple(VMEM for _ in outs),
+        out_specs=out_specs or tuple(VMEM for _ in outs),
         out_shape=tuple(outs),
         scratch_shapes=list(scratch),
         compiler_params=pltpu.CompilerParams(vmem_limit_bytes=limit),
@@ -53,12 +51,6 @@
 def split(value):
     high = value.astype(BF16)
     return high, (value - high.astype(F32)).astype(BF16)
-
-
-def code(value):
-    whole = jnp.round(value)
-    high = jnp.floor(whole * (1.0 / 256.0))
-    return high.astype(BF16), (whole - 256.0 * high).astype(BF16)
 
 
 def pack_body(wall_ref, pair_ref, theta_ref, out_ref, node_ref, near_ref, level_ref, ids_ref, plane_ref, sems):
@@ -123,17 +115,15 @@
         return carry
 
     lax.fori_loop(0, slots // 8, group, 0, unroll=8)
-    rows = iota((2 * slots, slots), 0)
-    wanted = (rows >> 2) * 2 + (rows & 1)
-    is_speed = ((rows >> 1) & 1) == 1
-    hit = send_ref[...] == wanted
-    pick_air = jnp.where(hit & jnp.logical_not(is_speed), 1.0, 0.0).astype(BF16)
-    pick_speed = jnp.where(hit & is_speed, 1.0, 0.0).astype(BF16)
-    air_high, air_low = code(air_ref[...] * (1.0 / air_step))
-    speed_high, speed_low = code(speed_ref[...] * (1.0 / coef_step))
-    out = 256.0 * (dot(pick_air, air_high) + dot(pick_speed, speed_high))
-    out = out + (dot(pick_air, air_low) + dot(pick_speed, speed_low))
-    out_ref[...] = out.astype(jnp.int32).astype(jnp.int16)
+    owners = slots // 2
+    wanted = iota((slots, slots), 0)
+    wanted = jnp.where(wanted < owners, 2 * wanted, 2 * (wanted - owners) + 1)
+    hit = jnp.where(send_ref[...] == wanted, 1.0, 0.0).astype(BF16)
+    both = jnp.concatenate([air_ref[...].astype(BF16), speed_ref[...].astype(BF16)], axis=1)
+    both = dot(hit, both)
+    for place in range(2):
+        out_ref[place] = both[place * owners : (place + 1) * owners, :128]
+        out_ref[2 + place] = both[place * owners : (place + 1) * owners, 128:]
 
 
 def reflect_body(pair_ref, recv_ref, block_ref, out_ref, add_ref, all_ref, src_ref):
@@ -159,8 +149,25 @@
     add_ref[...] = jnp.where(hot, 1.0, 0.0).astype(BF16)
 
 
+def cubics(g1, g2, g3, g4):
+    first = (g4, -(2.0 * g1 * g3 + g2 * g2), 3.0 * g1 * g1 * g2, -(g1 * g1) * (g1 * g1))
+    second = (g3, -2.0 * g1 * g2, g1 * g1 * g1)
+    third = (g2, -(g1 * g1))
+    return first, second, third, (g1,)
+
+
+def weighted(curves, rows):
+    totals = []
+    for power in range(4):
+        terms = [curve[power] if row is None else curve[power] * row
+                 for curve, row in zip(curves, rows) if power < len(curve)]
+        totals.append(functools.reduce(lambda x, y: x + y, terms))
+    return totals
+
+
 def wall_body(
-    class_ref, inverse_ref, wall_ref, take_ref, free_ref, rows_ref, gain_ref, resp_ref, take_out, back_out, lhs_ref,
+    class_ref, inverse_ref, wall_ref, take_ref,
+    free_ref, rows_ref, gain_ref, resp_ref, lam_ref, mix_ref, table_ref, take_out, back_out, kind_ref, lhs_ref,
 ):
     nodes = inverse_ref.shape[1]
     full = functools.partial(
@@ -181,6 +188,9 @@
         lhs_ref[c] = jnp.concatenate([high, high, low], axis=1)
         for k, power in enumerate((one, two, three, four)):
             resp_ref[c, k] = jnp.broadcast_to(power[:, 0:1], (nodes, 128))
+        curves = cubics(*[resp_ref[c, k, 0:1, :] for k in range(4)])
+        for power, value in enumerate(weighted(curves, [None] * 4)):
+            table_ref[4 * c + power : 4 * c + power + 1, :] = value
 
     owned = wall_ref.shape[1]
 
@@ -188,9 +198,11 @@
         base = pl.multiple_of(g * 8, 8)
         firsts = [[], [], [], [], []]
         gains = [[], [], [], []]
+        kinds = []
         for q in range(8):
             t = base + q
             kind = class_ref[0, t]
+            kinds.append(jnp.full((1, 128), kind, jnp.int32))
             state = wall_ref[0, t]
             high, low = split(state)
             result = dot(lhs_ref[kind], jnp.concatenate([high, low, high], axis=0))
@@ -205,61 +217,60 @@
             rows_ref[k, pl.ds(base, 8), :] = jnp.concatenate(firsts[k], axis=0)
         for k in range(4):
             gain_ref[k, pl.ds(base, 8), :] = jnp.concatenate(gains[k], axis=0)
+        kind_ref[pl.ds(base, 8), :] = jnp.concatenate(kinds, axis=0).astype(F32)
         return carry
 
     lax.fori_loop(0, owned // 8, tiles, 0, unroll=2)
+    curves = cubics(gain_ref[0], gain_ref[1], gain_ref[2], gain_ref[3])
+    for power, value in enumerate(weighted(curves, [None] * 4)):
+        lam_ref[power] = value
+    before = [rows_ref[3], rows_ref[0], rows_ref[1], rows_ref[2]]
+    for power, value in enumerate(weighted(curves, before)):
+        mix_ref[power] = value
     take = take_ref[...]
     col = column(take.astype(F32), owned).astype(jnp.int32)
-    place = (col >> 1) * 4 + (col & 1)
-    lanes = iota((owned, take_out.shape[1]), 1)
-    take_out[0:owned, :] = jnp.where(lanes == place, 1.0, 0.0).astype(BF16)
-    take_out[owned : 2 * owned, :] = jnp.where(lanes == place + 2, 1.0, 0.0).astype(BF16)
-    back_out[...] = jnp.where(iota((2 * owned, owned), 0) == take, 1.0, 0.0).astype(BF16)
-
-
-def force_body(recv_ref, take_ref, back_ref, refl_ref, add_ref, rows_ref, gain_ref, force_ref, out_ref):
+    lanes = iota((owned, 2 * owned), 1)
+    place = (col & 1) * owned + (col >> 1)
+    take_out[...] = jnp.where(lanes == place, 1.0, 0.0).astype(BF16)
+    wanted = iota((2 * owned, owned), 0)
+    wanted = jnp.where(wanted < owned, 2 * wanted, 2 * (wanted - owned) + 1)
+    back_out[...] = jnp.where(take == wanted, 1.0, 0.0).astype(BF16)
+
+
+def blend_body(refl_ref, add_ref, rows_ref, lam_ref, mix_ref, kind_ref, back_ref, fwd_ref, out_ref, rad_ref, list_ref):
+    parts, blocks = refl_ref.shape[0], refl_ref.shape[1]
     owned = add_ref.shape[0]
-    high, low = code(recv_ref[...].astype(jnp.int32).astype(F32))
-    both = 256.0 * dot(take_ref[...], high) + dot(take_ref[...], low)
-    air = air_step * both[0:owned]
-    coef = 0.5 + coef_step * both[owned : 2 * owned]
-    parts, blocks = refl_ref.shape[0], refl_ref.shape[1]
     rad = dot(add_ref[...], refl_ref[...].reshape(parts * blocks, 128))
-    g1, g2, g3, g4 = gain_ref[0], gain_ref[1], gain_ref[2], gain_ref[3]
-    f0 = wall_gain * (coef * (air - rows_ref[3]) + rad)
-    f1 = wall_gain * (coef * (air - (rows_ref[0] + g1 * f0)) + rad)
-    f2 = wall_gain * (coef * (air - (rows_ref[1] + (g2 * f0 + g1 * f1))) + rad)
-    f3 = wall_gain * (coef * (air - (rows_ref[2] + (g3 * f0 + g2 * f1 + g1 * f2))) + rad)
-    force_ref[0] = f0
-    force_ref[1] = f1
-    force_ref[2] = f2
-    force_ref[3] = f3
-    surface = rows_ref[4] + (g4 * f0 + g3 * f1 + g2 * f2 + g1 * f3)
-    high, low = split(surface)
-    out_ref[...] = dot(back_ref[...], high) + dot(back_ref[...], low)
+    rad_ref[...] = rad
+    quarter = wall_gain * rad
+    poly = [rows_ref[4] + quarter * lam_ref[0]]
+    for power in range(1, 4):
+        poly.append(quarter * lam_ref[power] - mix_ref[power - 1])
+    poly += [-mix_ref[3], kind_ref[...]]
+    placed = dot(back_ref[...], jnp.concatenate([p.astype(BF16) for p in poly], axis=1))
+    for t in range(4):
+        list_ref[pl.ds(t, owned, stride=16), :] = fwd_ref[t]
+    for place in range(2):
+        for m in range(6):
+            value = placed[place * owned : (place + 1) * owned, 128 * m : 128 * m + 128]
+            list_ref[pl.ds(4 + 6 * place + m, owned, stride=16), :] = value
+    out_ref[...] = list_ref[...].astype(BF16)
 
 
 def upwind(speed, centre, lower, upper):
     return jnp.maximum(speed, 0.0) * (centre - lower) + jnp.minimum(speed, 0.0) * (upper - centre)
 
 
-def finish_body(
-    class_ref, free_ref, force_ref, resp_ref, send_ref, speed_ref, theta_ref, wind_ref, eddy_ref, zhalo_ref,
-    before_ref, after_ref, out_ref, pick_ref, coef_ref, base_ref,
+def air_body(
+    theta_ref, wind_ref, eddy_ref, zhalo_ref, before_ref, after_ref, send_ref, speed_ref, base_ref, pick_ref, coef_ref
 ):
-    def tile(t, carry):
-        kind = class_ref[0, t]
-        value = free_ref[t]
-        for k in range(4):
-            value = value + resp_ref[kind, 3 - k] * force_ref[k, pl.ds(t, 1), :]
-        out_ref[0, t] = value
-        return carry
-
-    lax.fori_loop(0, free_ref.shape[0], tile, 0, unroll=4)
     slots = send_ref.shape[1]
-    slot_col = column(send_ref[...].astype(F32), slots)
-    pick_ref[...] = jnp.where(iota((slots, slots), 1).astype(F32) == slot_col, 1.0, 0.0).astype(BF16)
-    coef_ref[...] = jnp.where(slot_col >= 0.0, 0.5 + speed_ref[...], 0.0)
+    col = column(send_ref[...].astype(F32), slots)
+    live = col >= 0.0
+    whole = col.astype(jnp.int32)
+    place = jnp.where(live, (whole & 1) * (slots // 2) + (whole >> 1), -1)
+    pick_ref[...] = jnp.where(iota((slots, slots), 1) == place, 1.0, 0.0).astype(BF16)
+    coef_ref[...] = jnp.where(live, 0.5 + speed_ref[...], 0.0)
     level = lax.axis_index("gz")
     parts = zhalo_ref.shape[0]
 
@@ -287,11 +298,58 @@
         base_ref[k] = c - advect + eddy_ref[k] * laplace
 
 
-def deposit_body(recv_ref, pick_ref, air_ref, coef_ref, cell_ref, base_ref, out_ref, flux_ref, acc_ref):
+def close_body(
+    class_ref, recv_ref, take_ref, rows_ref, gain_ref, rad_ref, free_ref, resp_ref,
+    pick_ref, air_ref, coef_ref, table_ref, cell_ref, base_ref,
+    wall_hbm, out_ref, list_ref, force_ref, wall_ref, flux_ref, acc_ref, sem,
+):
+    list_ref[...] = recv_ref[...].astype(F32)
+    owned = rad_ref.shape[0]
+
+    def part(t):
+        return list_ref[pl.ds(t, owned, stride=16), :].astype(BF16)
+
+    taken = jnp.concatenate(
+        [jnp.concatenate([part(0), part(1)], axis=0), jnp.concatenate([part(2), part(3)], axis=0)], axis=1
+    )
+    taken = dot(take_ref[...], taken)
+    air = taken[:, :128]
+    quarter = wall_gain * (0.5 + taken[:, 128:])
+    rad = wall_gain * rad_ref[...]
+    g1, g2, g3 = gain_ref[0], gain_ref[1], gain_ref[2]
+    f0 = quarter * (air - rows_ref[3]) + rad
+    f1 = quarter * (air - (rows_ref[0] + g1 * f0)) + rad
+    f2 = quarter * (air - (rows_ref[1] + (g2 * f0 + g1 * f1))) + rad
+    f3 = quarter * (air - (rows_ref[2] + (g3 * f0 + g2 * f1 + g1 * f2))) + rad
+    force_ref[0] = f0
+    force_ref[1] = f1
+    force_ref[2] = f2
+    force_ref[3] = f3
+
+    def tile(t, carry):
+        kind = class_ref[0, t]
+        value = free_ref[t]
+        for k in range(4):
+            value = value + resp_ref[kind, 3 - k] * force_ref[k, pl.ds(t, 1), :]
+        wall_ref[0, t] = value
+        return carry
+
+    lax.fori_loop(0, owned, tile, 0, unroll=4)
+    copy = pltpu.make_async_copy(wall_ref, wall_hbm, sem)
+    copy.start()
+
     slots = cell_ref.shape[0]
-    high, low = split(recv_ref[...])
-    surface = dot(pick_ref[...], high) + dot(pick_ref[...], low)
-    flux_ref[...] = coef_ref[...] * (surface - air_ref[...])
+    back = [jnp.concatenate([part(4 + m), part(10 + m)], axis=0) for m in range(6)]
+    back = dot(pick_ref[...], jnp.concatenate(back, axis=1))
+    poly = [back[:, 128 * m : 128 * m + 128] for m in range(6)]
+    own_air, own_coef = air_ref[...], coef_ref[...]
+    h = wall_gain * own_coef
+    lam = jnp.zeros((slots, 128), F32)
+    for c in range(table_ref.shape[0] // 4):
+        one = [table_ref[4 * c + power : 4 * c + power + 1, :] for power in range(4)]
+        lam = jnp.where(poly[5] == float(c), one[0] + h * (one[1] + h * (one[2] + h * one[3])), lam)
+    surface = poly[0] + h * (poly[1] + h * (poly[2] + h * (poly[3] + h * poly[4]))) + h * own_air * lam
+    flux_ref[...] = own_coef * (surface - own_air)
     count = 8
     lanes = iota((128, count * 128), 0).astype(BF16)
     lines = iota((32, count * 128), 0).astype(BF16)
@@ -318,6 +376,7 @@
     heat = jnp.concatenate([heat[8 * q : 8 * q + 8] for q in range(4)], axis=1)
     for k in range(2):
         out_ref[k] = base_ref[k] + flux_gain * heat[4 * k : 4 * k + 4]
+    copy.wait()
 
 
 def on_device(
@@ -360,36 +419,35 @@
     )
     district = lax.all_to_all(payload, "gz", split_axis=0, concat_axis=0, tiled=True)
 
-    air, speed, send_list = call(
+    air, speed, forward = call(
         lookup_body,
         [VMEM] * 4,
-        [sds((slots, 128), F32), sds((slots, 128), F32), sds((2 * slots, 128), jnp.int16)],
+        [sds((slots, 128), F32), sds((slots, 128), F32), sds((4, slots // 2, 128), F32)],
         (potential_temp, wind_field, cells, tile_send),
         [pltpu.VMEM((32, 128), F32), pltpu.VMEM((32, 128), F32)],
         flops=2 * 48 * 256 * slots * 128,
     )
-    free, rows, gain, resp, take_pick, back_pick = call(
+    row4 = sds((4, owned, 128), F32)
+    free, rows, gain, resp, lam, mix, table, take_pick, back_pick, kind = call(
         wall_body,
         [SMEM] + [VMEM] * 3,
         [
             sds((owned, nodes, 128), F32),
             sds((5, owned, 128), F32),
-            sds((4, owned, 128), F32),
+            row4,
             sds((classes, 4, nodes, 128), F32),
-            sds((2 * owned, 2 * slots), BF16),
+            row4,
+            row4,
+            sds((4 * classes, 128), F32),
+            sds((owned, 2 * owned), BF16),
             sds((2 * owned, owned), BF16),
+            sds((owned, 128), F32),
         ],
         (wall_class, wall_inverse, wall_temp, tile_take),
         [pltpu.VMEM((classes, nodes + 16, 3 * nodes), BF16)],
         flops=2 * 48 * 96 * owned * 128,
     )
-    send_list, district, rows = lax.optimization_barrier((send_list, district, rows))
-    received = lax.all_to_all(send_list, "xy", split_axis=0, concat_axis=0, tiled=True)
-
-    last = xy_count - 1
-    before = lax.ppermute(potential_temp[:, 3:4, :], "xy", [(i, i + 1) for i in range(last)])
-    after = lax.ppermute(potential_temp[:, 0:1, :], "xy", [(i + 1, i) for i in range(last)])
-
+    district, forward, mix = lax.optimization_barrier((district, forward, mix))
     contrib, add_matrix = call(
         reflect_body,
         [SMEM, VMEM, VMEM],
@@ -397,37 +455,47 @@
         (refl_pair, district, refl_block),
         [pltpu.VMEM((parts * owned, 128), F32), pltpu.VMEM((blocks, 128), F32)],
     )
-    contrib, received = lax.optimization_barrier((contrib, received))
     reflected = lax.all_to_all(contrib, "gz", split_axis=0, concat_axis=0, tiled=True)
 
-    force, back_list = call(
-        force_body,
-        [VMEM] * 7,
-        [sds((4, owned, 128), F32), sds((2 * owned, 128), F32)],
-        (received, take_pick, back_pick, reflected, add_matrix, rows, gain),
-    )
-    returned = lax.all_to_all(back_list, "xy", split_axis=0, concat_axis=0, tiled=True)
-    wall_next, pick, coef, base = call(
-        finish_body,
-        [SMEM] + [VMEM] * 11,
+    last = xy_count - 1
+    before = lax.ppermute(potential_temp[:, 3:4, :], "xy", [(i, i + 1) for i in range(last)])
+    after = lax.ppermute(potential_temp[:, 0:1, :], "xy", [(i + 1, i) for i in range(last)])
+
+    send_list, rad = call(
+        blend_body,
+        [VMEM] * 8,
+        [sds((16 * xy_count, 128), BF16), sds((owned, 128), F32)],
+        (reflected, add_matrix, rows, lam, mix, kind, back_pick, forward),
+        [pltpu.VMEM((16 * xy_count, 128), F32)],
+    )
+    received = lax.all_to_all(send_list, "xy", split_axis=0, concat_axis=0, tiled=True)
+    base, pick, coef = call(
+        air_body,
+        [VMEM] * 8,
+        [sds(potential_temp.shape, F32), sds((slots, slots), BF16), sds((slots, 128), F32)],
+        (
+            potential_temp, wind_field, eddy_diff, district[:, owned + 16 : owned + 32, :], before, after,
+            tile_send, speed,
+        ),
+    )
+    wall_next, temp_next = call(
+        close_body,
+        [SMEM] + [VMEM] * 13,
+        [sds((1, owned, nodes, 128), F32), sds(potential_temp.shape, F32)],
+        (
+            wall_class, received, take_pick, rows, gain, rad, free, resp,
+            pick, air, coef, table, cells, base,
+        ),
         [
-            sds((1, owned, nodes, 128), F32),
-            sds((slots, slots), BF16),
-            sds((slots, 128), F32),
-            sds(potential_temp.shape, F32),
+            pltpu.VMEM((16 * xy_count, 128), F32),
+            pltpu.VMEM((4, owned, 128), F32),
+            pltpu.VMEM((1, owned, nodes, 128), F32),
+            pltpu.VMEM((slots, 128), F32),
+            pltpu.VMEM((128, 64), F32),
+            dma,
         ],
-        (
-            wall_class, free, force, resp, tile_send, speed, potential_temp, wind_field, eddy_diff,
-            district[:, owned + 16 : owned + 32, :], before, after,
-        ),
-    )
-    (temp_next,) = call(
-        deposit_body,
-        [VMEM] * 6,
-        [sds(potential_temp.shape, F32)],
-        (returned, pick, air, coef, cells, base),
-        [pltpu.VMEM((slots, 128), F32), pltpu.VMEM((128, 64), F32)],
         flops=2 * 64 * 128 * slots * 128,
+        out_specs=(pl.BlockSpec(memory_space=pl.ANY), VMEM),
     )
     return temp_next, wall_next
 
@@ -447,6 +515,4 @@
         P("xy", None, "gz"),
     )
     out_specs = (P("gz", "xy", None), P("gz", "xy", None, None))
-    return jax.shard_map(
-        on_device, mesh=mesh, in_specs=in_specs, out_specs=out_specs, check_vma=False
-    )
+    return jax.shard_map(on_device, mesh=mesh, in_specs=in_specs, out_specs=out_specs, check_vma=False)

time: 76.2 us -> 64 us (0.84)
  the two profiles are of different devices: /device:TPU:6 before, /device:TPU:1 now
where the time goes in v2:
time: 64 us; the launch traced here: 63.6 us
  starting transfers between devices  29.9 us (47%)
  Pallas kernels  11.5 us (18%)
  waiting for transfers between devices  10.3 us (16%)
  blocking collectives  9.68 us (15%)
  local copies, waits for them, and re-layouts  1.36 us (2%)
  between operations  0.83 us (1%)
    all_to_all x1, starting transfers between devices, on_device(): lax.all_to_all(send_list, 'xy', split_axis=0, concat_axis=0, tiled=True)  13.3 us
    pallas_call x7, Pallas kernels, call(): pl.pallas_call(body, in_specs=in_specs, out_specs=out_specs or tuple((VME...  11.5 us
    all_to_all x1, starting transfers between devices, on_device(): lax.all_to_all(payload, 'gz', split_axis=0, concat_axis=0, tiled=True)  11 us
    all_to_all x1, blocking collectives, on_device(): lax.all_to_all(contrib, 'gz', split_axis=0, concat_axis=0, tiled=True)  9.68 us
    all_to_all x1, waiting for transfers between devices, on_device(): lax.all_to_all(payload, 'gz', split_axis=0, concat_axis=0, tiled=True)  4.12 us
    all_to_all x1, waiting for transfers between devices, on_device(): lax.all_to_all(send_list, 'xy', split_axis=0, concat_axis=0, tiled=True)  3.73 us
    ppermute x1, starting transfers between devices, on_device(): lax.ppermute(potential_temp[:, 3:4, :], 'xy', [(i, i + 1) for i in range(...  3.2 us
    ppermute x1, waiting for transfers between devices, on_device(): lax.ppermute(potential_temp[:, 0:1, :], 'xy', [(i + 1, i) for i in range(...  2.48 us
  transfers between devices with their start and end apart: 4, of which 3 were waited for; matrix products, arithmetic and copies ran while one was open for 0% of the time, Pallas kernels for 7%

profile of v2, /device:TPU:1, one launch (start us, length us, event | category | flops | bytes accessed | tf_op | source)
XLA Modules:
  0.0 63.6 jit_solution(15867916085092663827)
XLA Ops:
  0.6 1.6 %shard_map.122 = bf16[8,96,128]{2,1,0:T(8,128)(2,1)} custom-call(f32[1,64,32,128]{3,2,1,0:T(8,128)} %wall_ref.3, s32[1,2,16]{2,1,0:T(2,128)} %pair_ref.3, f32[2,4,512]{2,1,0:T(4,128)} %theta_ref.5), custom_call_target="tpu_custom_call" | custom-call | bytes 1048576 | tf_op jit(solution)/shard_map/pallas_call | solution.py:27
  2.3 0.0 copy-start.3
  2.3 0.0 copy-start.8
  2.3 0.0 copy-start.9
  2.3 11.0 %all-to-all-start = ((bf16[8,96,128]{2,1,0:T(8,128)(2,1)}), bf16[8,96,128]{2,1,0:T(8,128)(2,1)S(1)}, u32[]{:S(2)}, u32[]{:S(2)}) async-start(bf16[8,96,128]{2,1,0:T(8,128)(2,1)} %shard_map.122), calls=%async_computation | async-start | bytes 393216 | tf_op jit(solution)/shard_map/all_to_all | solution.py:420
  13.3 0.0 copy-start.2
  13.3 0.0 copy-start.4
  13.3 0.0 copy-start.5
  13.4 2.7 %shard_map.124 = (f32[64,32,128]{2,1,0:T(8,128)S(1)}, f32[5,64,128]{2,1,0:T(8,128)S(1)}, f32[4,64,128]{2,1,0:T(8,128)S(1)}, f32[4,4,32,128]{3,2,1,0:T(8,128)S(1)...) custom-call(s32[1,64]{1,0:T(1,128)S(1)} %copy-done.8, ...), custom_call_target="tpu_custom_call" | custom-call | flops 75497472 | bytes 1048576 | tf_op jit(solution)/shard_map/pallas_call | solution.py:27
  16.1 0.6 copy-done.10
  16.7 1.4 %shard_map.123 = (f32[128,128]{1,0:T(8,128)S(1)}, f32[128,128]{1,0:T(8,128)S(1)}, f32[4,64,128]{2,1,0:T(8,128)S(1)}) custom-call(f32[2,4,512]{2,1,0:T(4,128)S(1)} %copy-done.2, f32[3,2,4,512]{3,2,1,0:T(4,128)S(1)} %copy-done.5, s32[128,128]{1,0:T(8,128)S(1)} %bitcast.4, s32[1,128]{1,0:T(1,128)S(1)} %copy-done.10), custom_call_target="tpu_custom_call" | custom-call | flops 402653184 | bytes 1048576 | tf_op jit(solution)/shard_map/pallas_call | solution.py:27
  18.2 4.1 %all-to-all-done.recv_ref = bf16[8,96,128]{2,1,0:T(8,128)(2,1)S(1)} async-done(((bf16[8,96,128]{2,1,0:T(8,128)(2,1)}), bf16[8,96,128]{2,1,0:T(8,128)(2,1)S(1)}, u32[]{:S(2)}, u32[]{:S(2)}) %all-to-all-start) | async-done | bytes 196640 | tf_op jit(solution)/shard_map/all_to_all | solution.py:420
  22.3 0.7 %copy-done.7 = s32[1,2,16]{2,1,0:T(2,128)S(1)} copy-done((s32[1,2,16]{2,1,0:T(2,128)S(1)}, s32[1,2,16]{2,1,0:T(2,128)}, u32[]{:S(2)}) %copy-start.7) | copy-done | bytes 152
  23.0 0.9 %shard_map.125 = (bf16[8,16,128]{2,1,0:T(8,128)(2,1)S(1)}, bf16[64,128]{1,0:T(8,128)(2,1)S(1)}) custom-call(s32[1,2,16]{2,1,0:T(2,128)S(1)} %copy-done.7, bf16[8,96,128]{2,1,0:T(8,128)(2,1)S(1)} %all-to-all-done.recv_ref, bf16[1,16,128,128]{3,2,1,0:T(8,128)(2,1)S(1)} %copy-done.1), custom_call_target="tpu_custom_call" | custom-call | bytes 1048576 | tf_op jit(solution)/shard_map/pallas_call | solution.py:27
  23.8 9.7 %all_to_all.21.refl_ref = bf16[8,16,128]{2,1,0:T(8,128)(2,1)S(1)} all-to-all(bf16[8,16,128]{2,1,0:T(8,128)(2,1)S(1)} %get-tuple-element.30), channel_id=1, replica_groups=mesh['xy'=64,'gz'=8] {'gz'}, dimensions={0} | all-to-all | bytes 65536 | tf_op jit(solution)/shard_map/all_to_all | solution.py:458
  33.5 1.1 %shard_map.126 = (bf16[1024,128]{1,0:T(8,128)(2,1)}, f32[64,128]{1,0:T(8,128)S(1)}) custom-call(bf16[8,16,128]{2,1,0:T(8,128)(2,1)S(1)} %all_to_all.21.refl_ref, bf16[64,128]{1,0:T(8,128)(2,1)S(1)} %get-tuple-element.31.add_ref, f32[5,64,128]{2,1,0:T(8,128)S(1)} %get-tuple-element.32.rows_ref, f32[4,64,128]{2,1,0:T(8,128)S(1)} %get-tuple-element.33.lam_ref, ...), custom_call_target="tpu_custom_call" | custom-call | bytes 1048576 | tf_op jit(solution)/shard_map/pallas_call | solution.py:27
  34.6 13.3 %all-to-all-start.2 = ((bf16[64,16,128]{2,1,0:T(8,128)(2,1)}), bf16[64,16,128]{2,1,0:T(8,128)(2,1)S(1)}, u32[]{:S(2)}, u32[]{:S(2)}) async-start(bf16[64,16,128]{2,1,0:T(8,128)(2,1)} %bitcast.1), calls=%async_computation.2 | async-start | bytes 524288 | tf_op jit(solution)/shard_map/all_to_all | solution.py:471
  48.0 2.4 %collective-permute-start.1 = (f32[2,1,512]{2,1,0:T(1,128)S(1)}, f32[2,1,512]{2,1,0:T(1,128)S(1)}, u32[]{:S(2)}, u32[]{:S(2)}) collective-permute-start(f32[2,1,512]{2,1,0:T(1,128)S(1)} %get-tuple-element.52), channel_id=1, source_target_pairs={{8,0},{16,8},{24,16},{32,24},{40,32},{48,40},{56,48},{64,56},{72,6... | collective-permute-start | bytes 12296 | tf_op jit(solution)/shard_map/ppermute | solution.py:462
  50.3 0.0 copy-start.6
  50.4 3.2 %collective-permute-start = (f32[2,1,512]{2,1,0:T(1,128)S(1)}, f32[2,1,512]{2,1,0:T(1,128)S(1)}, u32[]{:S(2)}, u32[]{:S(2)}) collective-permute-start(f32[2,1,512]{2,1,0:T(1,128)S(1)} %get-tuple-element.53), channel_id=1, source_target_pairs={{0,8},{8,16},{16,24},{24,32},{32,40},{40,48},{48,56},{56,64},{64,7... | collective-permute-start | bytes 12296 | tf_op jit(solution)/shard_map/ppermute | solution.py:461
  53.6 2.5 %collective-permute-done.1.after_ref = f32[2,1,512]{2,1,0:T(1,128)S(1)} collective-permute-done((f32[2,1,512]{2,1,0:T(1,128)S(1)}, f32[2,1,512]{2,1,0:T(1,128)S(1)}, u32[]{:S(2)}, u32[]{:S(2)}) %collective-permute-start.1) | collective-permute-done | bytes 4128 | tf_op jit(solution)/shard_map/ppermute | solution.py:462
  56.1 0.1 shard_map.127
  56.2 3.7 %all-to-all-done.2 = bf16[64,16,128]{2,1,0:T(8,128)(2,1)S(1)} async-done(((bf16[64,16,128]{2,1,0:T(8,128)(2,1)}), bf16[64,16,128]{2,1,0:T(8,128)(2,1)S(1)}, u32[]{:S(2)}, u32[]{:S(2)}) %all-to-all-start.2) | async-done | bytes 262176 | tf_op jit(solution)/shard_map/all_to_all | solution.py:471
  59.9 3.6 %shard_map.128 = (f32[1,64,32,128]{3,2,1,0:T(8,128)}, f32[2,4,512]{2,1,0:T(4,128)}) custom-call(s32[1,64]{1,0:T(1,128)S(1)} %copy-done.8, bf16[1024,128]{1,0:T(8,128)(2,1)S(1)} %bitcast.3, bf16[64,128]{1,0:T(8,128)(2,1)S(1)} %get-tuple-element.39.take_ref, f32[5,64,128]{2,1,0:T(8,128)S(1)} %get-tuple-element.32.rows_ref, ...), custom_call_target="tpu_custom_call" | custom-call | flops 268435456 | bytes 1048576 | tf_op jit(solution)/shard_map/pallas_call | solution.py:27
  (16 shorter events, 0.0 us)
Async XLA Ops:
  0.6 12.7 %copy-start = (f32[1,64,32,128]{3,2,1,0:T(8,128)S(1)}, f32[1,64,32,128]{3,2,1,0:T(8,128)}, u32[]{:S(2)}) copy-start(f32[1,64,32,128]{3,2,1,0:T(8,128)} %wall_ref.3) | copy-start | bytes 3145732
  2.3 11.0 %copy-start.3 = (f32[4,32,32]{2,1,0:T(8,128)S(1)}, f32[4,32,32]{2,1,0:T(8,128)}, u32[]{:S(2)}) copy-start(f32[4,32,32]{2,1,0:T(8,128)} %inverse_ref.1) | copy-start | bytes 49156
  2.3 11.0 %copy-start.8 = (s32[1,64]{1,0:T(1,128)S(1)}, s32[1,64]{1,0:T(1,128)}, u32[]{:S(2)}) copy-start(s32[1,64]{1,0:T(1,128)} %class_ref.3) | copy-start | bytes 772
  2.3 11.0 %copy-start.9 = (s32[1,64]{1,0:T(1,128)S(1)}, s32[1,64]{1,0:T(1,128)}, u32[]{:S(2)}) copy-start(s32[1,64]{1,0:T(1,128)} %take_ref.1) | copy-start | bytes 772
  2.3 20.0 %all-to-all-start = ((bf16[8,96,128]{2,1,0:T(8,128)(2,1)}), bf16[8,96,128]{2,1,0:T(8,128)(2,1)S(1)}, u32[]{:S(2)}, u32[]{:S(2)}) async-start(bf16[8,96,128]{2,1,0:T(8,128)(2,1)} %shard_map.122), calls=%async_computation | async-start | bytes 393216 | tf_op jit(solution)/shard_map/all_to_all | solution.py:420
  13.3 2.8 %copy-start.2 = (f32[2,4,512]{2,1,0:T(4,128)S(1)}, f32[2,4,512]{2,1,0:T(4,128)}, u32[]{:S(2)}) copy-start(f32[2,4,512]{2,1,0:T(4,128)} %theta_ref.5) | copy-start | bytes 49156
  13.3 2.8 %copy-start.4 = (s32[1,128,128]{2,1,0:T(8,128)S(1)}, s32[1,128,128]{2,1,0:T(8,128)}, u32[]{:S(2)}) copy-start(s32[1,128,128]{2,1,0:T(8,128)} %param.14) | copy-start | bytes 196612
  13.3 2.8 %copy-start.5 = (f32[3,2,4,512]{3,2,1,0:T(4,128)S(1)}, f32[3,2,4,512]{3,2,1,0:T(4,128)}, u32[]{:S(2)}) copy-start(f32[3,2,4,512]{3,2,1,0:T(4,128)} %wind_ref.3) | copy-start | bytes 147460
  16.1 0.7 %copy-start.10 = (s32[1,128]{1,0:T(1,128)S(1)}, s32[1,128]{1,0:T(1,128)}, u32[]{:S(2)}) copy-start(s32[1,128]{1,0:T(1,128)} %send_ref.3) | copy-start | bytes 1540
  16.7 5.5 %copy-start.1 = (bf16[1,16,128,128]{3,2,1,0:T(8,128)(2,1)S(1)}, bf16[1,16,128,128]{3,2,1,0:T(8,128)(2,1)}, u32[]{:S(2)}) copy-start(bf16[1,16,128,128]{3,2,1,0:T(8,128)(2,1)} %block_ref.1) | copy-start | bytes 1572868
  22.3 0.7 %copy-start.7 = (s32[1,2,16]{2,1,0:T(2,128)S(1)}, s32[1,2,16]{2,1,0:T(2,128)}, u32[]{:S(2)}) copy-start(s32[1,2,16]{2,1,0:T(2,128)} %pair_ref.3) | copy-start | bytes 388
  34.6 25.3 %all-to-all-start.2 = ((bf16[64,16,128]{2,1,0:T(8,128)(2,1)}), bf16[64,16,128]{2,1,0:T(8,128)(2,1)S(1)}, u32[]{:S(2)}, u32[]{:S(2)}) async-start(bf16[64,16,128]{2,1,0:T(8,128)(2,1)} %bitcast.1), calls=%async_computation.2 | async-start | bytes 524288 | tf_op jit(solution)/shard_map/all_to_all | solution.py:471
  48.0 8.1 %collective-permute-start.1 = (f32[2,1,512]{2,1,0:T(1,128)S(1)}, f32[2,1,512]{2,1,0:T(1,128)S(1)}, u32[]{:S(2)}, u32[]{:S(2)}) collective-permute-start(f32[2,1,512]{2,1,0:T(1,128)S(1)} %get-tuple-element.52), channel_id=1, source_target_pairs={{8,0},{16,8},{24,16},{32,24},{40,32},{48,40},{56,48},{64,56},{72,6... | collective-permute-start | bytes 12296 | tf_op jit(solution)/shard_map/ppermute | solution.py:462
  50.3 5.7 %copy-start.6 = (f32[2,4,512]{2,1,0:T(4,128)S(1)}, f32[2,4,512]{2,1,0:T(4,128)}, u32[]{:S(2)}) copy-start(f32[2,4,512]{2,1,0:T(4,128)} %eddy_ref.1) | copy-start | bytes 49156
  50.4 5.7 %collective-permute-start = (f32[2,1,512]{2,1,0:T(1,128)S(1)}, f32[2,1,512]{2,1,0:T(1,128)S(1)}, u32[]{:S(2)}, u32[]{:S(2)}) collective-permute-start(f32[2,1,512]{2,1,0:T(1,128)S(1)} %get-tuple-element.53), channel_id=1, source_target_pairs={{0,8},{8,16},{16,24},{24,32},{32,40},{40,48},{48,56},{56,64},{64,7... | collective-permute-start | bytes 12296 | tf_op jit(solution)/shard_map/ppermute | solution.py:461

commit v3 on v2

--- a/solution.py
+++ b/solution.py
@@ -84,7 +84,11 @@
         out_ref[dest, owned + 16 : owned + 32, :] = (up + down).astype(BF16)
 
 
-def lookup_body(theta_ref, wind_ref, cell_ref, send_ref, air_ref, speed_ref, out_ref, theta_tab, speed_tab):
+def lookup_body(
+    theta_ref, wind_ref, cell_ref, send_ref, pair_ref,
+    air_ref, speed_ref, out_ref, pair_out, theta_tab, speed_tab,
+):
+    pair_out[...] = pair_ref[...]
     theta = jnp.concatenate([theta_ref[0], theta_ref[1]], axis=0)
     speed = jnp.zeros_like(theta)
     for d in range(3):
@@ -334,7 +338,7 @@
         wall_ref[0, t] = value
         return carry
 
-    lax.fori_loop(0, owned, tile, 0, unroll=4)
+    lax.fori_loop(0, owned, tile, 0, unroll=8)
     copy = pltpu.make_async_copy(wall_ref, wall_hbm, sem)
     copy.start()
 
@@ -370,7 +374,7 @@
         acc_ref[...] += dot(hot, placed, ((1,), (1,)))
         return carry
 
-    lax.fori_loop(0, slots // count, group, 0, unroll=8)
+    lax.fori_loop(0, slots // count, group, 0, unroll=16)
     heat = acc_ref[...].T
     heat = heat[0:32] + heat[32:64]
     heat = jnp.concatenate([heat[8 * q : 8 * q + 8] for q in range(4)], axis=1)
@@ -419,11 +423,16 @@
     )
     district = lax.all_to_all(payload, "gz", split_axis=0, concat_axis=0, tiled=True)
 
-    air, speed, forward = call(
+    air, speed, forward, pair = call(
         lookup_body,
-        [VMEM] * 4,
-        [sds((slots, 128), F32), sds((slots, 128), F32), sds((4, slots // 2, 128), F32)],
-        (potential_temp, wind_field, cells, tile_send),
+        [VMEM] * 5,
+        [
+            sds((slots, 128), F32),
+            sds((slots, 128), F32),
+            sds((4, slots // 2, 128), F32),
+            sds(refl_pair.shape, jnp.int32),
+        ],
+        (potential_temp, wind_field, cells, tile_send, refl_pair),
         [pltpu.VMEM((32, 128), F32), pltpu.VMEM((32, 128), F32)],
         flops=2 * 48 * 256 * slots * 128,
     )
@@ -452,7 +461,7 @@
         reflect_body,
         [SMEM, VMEM, VMEM],
         [sds((parts, blocks, 128), BF16), sds((owned, 128), BF16)],
-        (refl_pair, district, refl_block),
+        (pair, district, refl_block),
         [pltpu.VMEM((parts * owned, 128), F32), pltpu.VMEM((blocks, 128), F32)],
     )
     reflected = lax.all_to_all(contrib, "gz", split_axis=0, concat_axis=0, tiled=True)
@@ -515,4 +524,6 @@
         P("xy", None, "gz"),
     )
     out_specs = (P("gz", "xy", None), P("gz", "xy", None, None))
-    return jax.shard_map(on_device, mesh=mesh, in_specs=in_specs, out_specs=out_specs, check_vma=False)
+    return jax.shard_map(
+        on_device, mesh=mesh, in_specs=in_specs, out_specs=out_specs, check_vma=False
+    )

time: 64 us -> 63.7 us (level)
  local copies, waits for them, and re-layouts: 1.36 us -> 0.7 us
    unnamed x22, local copies, waits for them, and re-layouts: 1.35 us -> 0.69 us
where the time goes in v3:
time: 63.7 us; the launch traced here: 63.3 us
  starting transfers between devices  29.9 us (47%)
  Pallas kernels  11.9 us (19%)
  waiting for transfers between devices  10.3 us (16%)
  blocking collectives  9.68 us (15%)
  between operations  0.84 us (1%)
  local copies, waits for them, and re-layouts  0.7 us (1%)
    all_to_all x1, starting transfers between devices, on_device(): lax.all_to_all(send_list, 'xy', split_axis=0, concat_axis=0, tiled=True)  13.3 us
    pallas_call x7, Pallas kernels, call(): pl.pallas_call(body, in_specs=in_specs, out_specs=out_specs or tuple((VME...  11.9 us
    all_to_all x1, starting transfers between devices, on_device(): lax.all_to_all(payload, 'gz', split_axis=0, concat_axis=0, tiled=True)  11 us
    all_to_all x1, blocking collectives, on_device(): lax.all_to_all(contrib, 'gz', split_axis=0, concat_axis=0, tiled=True)  9.68 us
    all_to_all x1, waiting for transfers between devices, on_device(): lax.all_to_all(payload, 'gz', split_axis=0, concat_axis=0, tiled=True)  4.09 us
    all_to_all x1, waiting for transfers between devices, on_device(): lax.all_to_all(send_list, 'xy', split_axis=0, concat_axis=0, tiled=True)  3.73 us
    ppermute x1, starting transfers between devices, on_device(): lax.ppermute(potential_temp[:, 3:4, :], 'xy', [(i, i + 1) for i in range(...  3.2 us
    ppermute x1, waiting for transfers between devices, on_device(): lax.ppermute(potential_temp[:, 0:1, :], 'xy', [(i + 1, i) for i in range(...  2.48 us
  transfers between devices with their start and end apart: 4, of which 3 were waited for; matrix products, arithmetic and copies ran while one was open for 0% of the time, Pallas kernels for 7%

profile of v3, /device:TPU:1, one launch (start us, length us, event | category | flops | bytes accessed | tf_op | source)
XLA Modules:
  0.0 63.3 jit_solution(2538466826089485293)
XLA Ops:
  0.6 1.6 %shard_map.123 = bf16[8,96,128]{2,1,0:T(8,128)(2,1)} custom-call(f32[1,64,32,128]{3,2,1,0:T(8,128)} %wall_ref.3, s32[1,2,16]{2,1,0:T(2,128)} %pair_ref.3, f32[2,4,512]{2,1,0:T(4,128)} %theta_ref.5), custom_call_target="tpu_custom_call" | custom-call | bytes 1048576 | tf_op jit(solution)/shard_map/pallas_call | solution.py:27
  2.3 0.0 copy-start.3
  2.3 0.0 copy-start.7
  2.3 0.0 copy-start.9
  2.3 11.0 %all-to-all-start = ((bf16[8,96,128]{2,1,0:T(8,128)(2,1)}), bf16[8,96,128]{2,1,0:T(8,128)(2,1)S(1)}, u32[]{:S(2)}, u32[]{:S(2)}) async-start(bf16[8,96,128]{2,1,0:T(8,128)(2,1)} %shard_map.123), calls=%async_computation | async-start | bytes 393216 | tf_op jit(solution)/shard_map/all_to_all | solution.py:424
  13.3 0.0 copy-start.2
  13.3 0.0 copy-start.4
  13.3 0.0 copy-start.5
  13.4 2.7 %shard_map.124 = (f32[64,32,128]{2,1,0:T(8,128)S(1)}, f32[5,64,128]{2,1,0:T(8,128)S(1)}, f32[4,64,128]{2,1,0:T(8,128)S(1)}, f32[4,4,32,128]{3,2,1,0:T(8,128)S(1)...) custom-call(s32[1,64]{1,0:T(1,128)S(1)} %copy-done.7, ...), custom_call_target="tpu_custom_call" | custom-call | flops 75497472 | bytes 1048576 | tf_op jit(solution)/shard_map/pallas_call | solution.py:27
  16.1 0.0 copy-start.8
  16.1 0.0 copy-start.10
  16.1 0.6 copy-done.8
  16.8 1.4 %shard_map.122 = (f32[128,128]{1,0:T(8,128)S(1)}, f32[128,128]{1,0:T(8,128)S(1)}, f32[4,64,128]{2,1,0:T(8,128)S(1)}, s32[1,2,16]{2,1,0:T(2,128)S(1)}) custom-call(f32[2,4,512]{2,1,0:T(4,128)S(1)} %copy-done.2, f32[3,2,4,512]{3,2,1,0:T(4,128)S(1)} %copy-done.5, s32[128,128]{1,0:T(8,128)S(1)} %bitcast.4, s32[1,128]{1,0:T(1,128)S(1)} %copy-done.10, ...), custom_call_target="tpu_custom_call" | custom-call | flops 402653184 | bytes 1048576 | tf_op jit(solution)/shard_map/pallas_call | solution.py:27
  18.2 4.1 %all-to-all-done.recv_ref = bf16[8,96,128]{2,1,0:T(8,128)(2,1)S(1)} async-done(((bf16[8,96,128]{2,1,0:T(8,128)(2,1)}), bf16[8,96,128]{2,1,0:T(8,128)(2,1)S(1)}, u32[]{:S(2)}, u32[]{:S(2)}) %all-to-all-start) | async-done | bytes 196640 | tf_op jit(solution)/shard_map/all_to_all | solution.py:424
  22.3 0.9 %shard_map.125 = (bf16[8,16,128]{2,1,0:T(8,128)(2,1)S(1)}, bf16[64,128]{1,0:T(8,128)(2,1)S(1)}) custom-call(s32[1,2,16]{2,1,0:T(2,128)S(1)} %get-tuple-element.28.pair_ref, bf16[8,96,128]{2,1,0:T(8,128)(2,1)S(1)} %all-to-all-done.recv_ref, bf16[1,16,128,128]{3,2,1,0:T(8,128)(2,1)S(1)} %copy-done.1), custom_call_target="tpu_custom_call" | custom-call | bytes 1048576 | tf_op jit(solution)/shard_map/pallas_call | solution.py:27
  23.2 9.7 %all_to_all.21.refl_ref = bf16[8,16,128]{2,1,0:T(8,128)(2,1)S(1)} all-to-all(bf16[8,16,128]{2,1,0:T(8,128)(2,1)S(1)} %get-tuple-element.32), channel_id=1, replica_groups=mesh['xy'=64,'gz'=8] {'gz'}, dimensions={0} | all-to-all | bytes 65536 | tf_op jit(solution)/shard_map/all_to_all | solution.py:467
  32.9 1.1 %shard_map.126 = (bf16[1024,128]{1,0:T(8,128)(2,1)}, f32[64,128]{1,0:T(8,128)S(1)}) custom-call(bf16[8,16,128]{2,1,0:T(8,128)(2,1)S(1)} %all_to_all.21.refl_ref, bf16[64,128]{1,0:T(8,128)(2,1)S(1)} %get-tuple-element.33.add_ref, f32[5,64,128]{2,1,0:T(8,128)S(1)} %get-tuple-element.34.rows_ref, f32[4,64,128]{2,1,0:T(8,128)S(1)} %get-tuple-element.35.lam_ref, ...), custom_call_target="tpu_custom_call" | custom-call | bytes 1048576 | tf_op jit(solution)/shard_map/pallas_call | solution.py:27
  34.0 13.3 %all-to-all-start.2 = ((bf16[64,16,128]{2,1,0:T(8,128)(2,1)}), bf16[64,16,128]{2,1,0:T(8,128)(2,1)S(1)}, u32[]{:S(2)}, u32[]{:S(2)}) async-start(bf16[64,16,128]{2,1,0:T(8,128)(2,1)} %bitcast.1), calls=%async_computation.2 | async-start | bytes 524288 | tf_op jit(solution)/shard_map/all_to_all | solution.py:480
  47.3 2.4 %collective-permute-start.1 = (f32[2,1,512]{2,1,0:T(1,128)S(1)}, f32[2,1,512]{2,1,0:T(1,128)S(1)}, u32[]{:S(2)}, u32[]{:S(2)}) collective-permute-start(f32[2,1,512]{2,1,0:T(1,128)S(1)} %get-tuple-element.54), channel_id=1, source_target_pairs={{8,0},{16,8},{24,16},{32,24},{40,32},{48,40},{56,48},{64,56},{72,6... | collective-permute-start | bytes 12296 | tf_op jit(solution)/shard_map/ppermute | solution.py:471
  49.7 3.2 %collective-permute-start = (f32[2,1,512]{2,1,0:T(1,128)S(1)}, f32[2,1,512]{2,1,0:T(1,128)S(1)}, u32[]{:S(2)}, u32[]{:S(2)}) collective-permute-start(f32[2,1,512]{2,1,0:T(1,128)S(1)} %get-tuple-element.55), channel_id=1, source_target_pairs={{0,8},{8,16},{16,24},{24,32},{32,40},{40,48},{48,56},{56,64},{64,7... | collective-permute-start | bytes 12296 | tf_op jit(solution)/shard_map/ppermute | solution.py:470
  52.9 2.5 %collective-permute-done.1.after_ref = f32[2,1,512]{2,1,0:T(1,128)S(1)} collective-permute-done((f32[2,1,512]{2,1,0:T(1,128)S(1)}, f32[2,1,512]{2,1,0:T(1,128)S(1)}, u32[]{:S(2)}, u32[]{:S(2)}) %collective-permute-start.1) | collective-permute-done | bytes 4128 | tf_op jit(solution)/shard_map/ppermute | solution.py:471
  55.4 0.1 shard_map.127
  55.5 3.7 %all-to-all-done.2 = bf16[64,16,128]{2,1,0:T(8,128)(2,1)S(1)} async-done(((bf16[64,16,128]{2,1,0:T(8,128)(2,1)}), bf16[64,16,128]{2,1,0:T(8,128)(2,1)S(1)}, u32[]{:S(2)}, u32[]{:S(2)}) %all-to-all-start.2) | async-done | bytes 262176 | tf_op jit(solution)/shard_map/all_to_all | solution.py:480
  59.2 4.1 %shard_map.128 = (f32[1,64,32,128]{3,2,1,0:T(8,128)}, f32[2,4,512]{2,1,0:T(4,128)}) custom-call(s32[1,64]{1,0:T(1,128)S(1)} %copy-done.7, bf16[1024,128]{1,0:T(8,128)(2,1)S(1)} %bitcast.3, bf16[64,128]{1,0:T(8,128)(2,1)S(1)} %get-tuple-element.41.take_ref, f32[5,64,128]{2,1,0:T(8,128)S(1)} %get-tuple-element.34.rows_ref, ...), custom_call_target="tpu_custom_call" | custom-call | flops 268435456 | bytes 1048576 | tf_op jit(solution)/shard_map/pallas_call | solution.py:27
  (16 shorter events, 0.0 us)
Async XLA Ops:
  0.6 12.7 %copy-start = (f32[1,64,32,128]{3,2,1,0:T(8,128)S(1)}, f32[1,64,32,128]{3,2,1,0:T(8,128)}, u32[]{:S(2)}) copy-start(f32[1,64,32,128]{3,2,1,0:T(8,128)} %wall_ref.3) | copy-start | bytes 3145732
  2.3 11.0 %copy-start.3 = (f32[4,32,32]{2,1,0:T(8,128)S(1)}, f32[4,32,32]{2,1,0:T(8,128)}, u32[]{:S(2)}) copy-start(f32[4,32,32]{2,1,0:T(8,128)} %inverse_ref.1) | copy-start | bytes 49156
  2.3 11.0 %copy-start.7 = (s32[1,64]{1,0:T(1,128)S(1)}, s32[1,64]{1,0:T(1,128)}, u32[]{:S(2)}) copy-start(s32[1,64]{1,0:T(1,128)} %class_ref.3) | copy-start | bytes 772
  2.3 11.0 %copy-start.9 = (s32[1,64]{1,0:T(1,128)S(1)}, s32[1,64]{1,0:T(1,128)}, u32[]{:S(2)}) copy-start(s32[1,64]{1,0:T(1,128)} %take_ref.1) | copy-start | bytes 772
  2.3 20.0 %all-to-all-start = ((bf16[8,96,128]{2,1,0:T(8,128)(2,1)}), bf16[8,96,128]{2,1,0:T(8,128)(2,1)S(1)}, u32[]{:S(2)}, u32[]{:S(2)}) async-start(bf16[8,96,128]{2,1,0:T(8,128)(2,1)} %shard_map.123), calls=%async_computation | async-start | bytes 393216 | tf_op jit(solution)/shard_map/all_to_all | solution.py:424
  13.3 2.8 %copy-start.2 = (f32[2,4,512]{2,1,0:T(4,128)S(1)}, f32[2,4,512]{2,1,0:T(4,128)}, u32[]{:S(2)}) copy-start(f32[2,4,512]{2,1,0:T(4,128)} %theta_ref.5) | copy-start | bytes 49156
  13.3 2.8 %copy-start.4 = (s32[1,128,128]{2,1,0:T(8,128)S(1)}, s32[1,128,128]{2,1,0:T(8,128)}, u32[]{:S(2)}) copy-start(s32[1,128,128]{2,1,0:T(8,128)} %param.14) | copy-start | bytes 196612
  13.3 2.8 %copy-start.5 = (f32[3,2,4,512]{3,2,1,0:T(4,128)S(1)}, f32[3,2,4,512]{3,2,1,0:T(4,128)}, u32[]{:S(2)}) copy-start(f32[3,2,4,512]{3,2,1,0:T(4,128)} %wind_ref.3) | copy-start | bytes 147460
  16.1 0.7 %copy-start.8 = (s32[1,2,16]{2,1,0:T(2,128)S(1)}, s32[1,2,16]{2,1,0:T(2,128)}, u32[]{:S(2)}) copy-start(s32[1,2,16]{2,1,0:T(2,128)} %pair_ref.3) | copy-start | bytes 388
  16.1 0.7 %copy-start.10 = (s32[1,128]{1,0:T(1,128)S(1)}, s32[1,128]{1,0:T(1,128)}, u32[]{:S(2)}) copy-start(s32[1,128]{1,0:T(1,128)} %send_ref.3) | copy-start | bytes 1540
  16.8 5.5 %copy-start.1 = (bf16[1,16,128,128]{3,2,1,0:T(8,128)(2,1)S(1)}, bf16[1,16,128,128]{3,2,1,0:T(8,128)(2,1)}, u32[]{:S(2)}) copy-start(bf16[1,16,128,128]{3,2,1,0:T(8,128)(2,1)} %block_ref.1) | copy-start | bytes 1572868
  34.0 25.3 %all-to-all-start.2 = ((bf16[64,16,128]{2,1,0:T(8,128)(2,1)}), bf16[64,16,128]{2,1,0:T(8,128)(2,1)S(1)}, u32[]{:S(2)}, u32[]{:S(2)}) async-start(bf16[64,16,128]{2,1,0:T(8,128)(2,1)} %bitcast.1), calls=%async_computation.2 | async-start | bytes 524288 | tf_op jit(solution)/shard_map/all_to_all | solution.py:480
  47.3 8.1 %collective-permute-start.1 = (f32[2,1,512]{2,1,0:T(1,128)S(1)}, f32[2,1,512]{2,1,0:T(1,128)S(1)}, u32[]{:S(2)}, u32[]{:S(2)}) collective-permute-start(f32[2,1,512]{2,1,0:T(1,128)S(1)} %get-tuple-element.54), channel_id=1, source_target_pairs={{8,0},{16,8},{24,16},{32,24},{40,32},{48,40},{56,48},{64,56},{72,6... | collective-permute-start | bytes 12296 | tf_op jit(solution)/shard_map/ppermute | solution.py:471
  49.7 5.7 %copy-start.6 = (f32[2,4,512]{2,1,0:T(4,128)S(1)}, f32[2,4,512]{2,1,0:T(4,128)}, u32[]{:S(2)}) copy-start(f32[2,4,512]{2,1,0:T(4,128)} %eddy_ref.1) | copy-start | bytes 49156
  49.7 5.7 %collective-permute-start = (f32[2,1,512]{2,1,0:T(1,128)S(1)}, f32[2,1,512]{2,1,0:T(1,128)S(1)}, u32[]{:S(2)}, u32[]{:S(2)}) collective-permute-start(f32[2,1,512]{2,1,0:T(1,128)S(1)} %get-tuple-element.55), channel_id=1, source_target_pairs={{0,8},{8,16},{16,24},{24,32},{32,40},{40,48},{48,56},{56,64},{64,7... | collective-permute-start | bytes 12296 | tf_op jit(solution)/shard_map/ppermute | solution.py:470

commit v4 on v3

--- a/solution.py
+++ b/solution.py
@@ -266,7 +266,7 @@
 
 
 def air_body(
-    theta_ref, wind_ref, eddy_ref, zhalo_ref, before_ref, after_ref, send_ref, speed_ref, base_ref, pick_ref, coef_ref
+    theta_ref, wind_ref, eddy_ref, zhalo_ref, near_ref, far_ref, send_ref, speed_ref, base_ref, pick_ref, coef_ref
 ):
     slots = send_ref.shape[1]
     col = column(send_ref[...].astype(F32), slots)
@@ -285,12 +285,15 @@
 
     below = plane(level - 1, level > 0)
     above = plane(level + 1, level < parts - 1)
+    even = lax.axis_index("xy") % 2 == 0
     for k in range(2):
+        before = jnp.where(even, far_ref[k], near_ref[k])
+        after = jnp.where(even, near_ref[k], far_ref[k])
         c = theta_ref[k]
         lower_z = theta_ref[0] if k else below
         upper_z = above if k else theta_ref[1]
-        lower_x = jnp.concatenate([before_ref[k], c[0:3]], axis=0)
-        upper_x = jnp.concatenate([c[1:4], after_ref[k]], axis=0)
+        lower_x = jnp.concatenate([before, c[0:3]], axis=0)
+        upper_x = jnp.concatenate([c[1:4], after], axis=0)
         lower_y = jnp.concatenate([c[:, -1:], c[:, :-1]], axis=1)
         upper_y = jnp.concatenate([c[:, 1:], c[:, :1]], axis=1)
         advect = (
@@ -338,7 +341,7 @@
         wall_ref[0, t] = value
         return carry
 
-    lax.fori_loop(0, owned, tile, 0, unroll=8)
+    lax.fori_loop(0, owned, tile, 0, unroll=4)
     copy = pltpu.make_async_copy(wall_ref, wall_hbm, sem)
     copy.start()
 
@@ -374,7 +377,7 @@
         acc_ref[...] += dot(hot, placed, ((1,), (1,)))
         return carry
 
-    lax.fori_loop(0, slots // count, group, 0, unroll=16)
+    lax.fori_loop(0, slots // count, group, 0, unroll=8)
     heat = acc_ref[...].T
     heat = heat[0:32] + heat[32:64]
     heat = jnp.concatenate([heat[8 * q : 8 * q + 8] for q in range(4)], axis=1)
@@ -466,9 +469,12 @@
     )
     reflected = lax.all_to_all(contrib, "gz", split_axis=0, concat_axis=0, tiled=True)
 
-    last = xy_count - 1
-    before = lax.ppermute(potential_temp[:, 3:4, :], "xy", [(i, i + 1) for i in range(last)])
-    after = lax.ppermute(potential_temp[:, 0:1, :], "xy", [(i + 1, i) for i in range(last)])
+    even = lax.axis_index("xy") % 2 == 0
+    first_row, last_row = potential_temp[:, 0:1, :], potential_temp[:, 3:4, :]
+    mates = [(i, i + 1) for i in range(0, xy_count, 2)]
+    others = [(i, i + 1) for i in range(1, xy_count - 1, 2)]
+    near = lax.ppermute(jnp.where(even, last_row, first_row), "xy", mates + [(j, i) for i, j in mates])
+    far = lax.ppermute(jnp.where(even, first_row, last_row), "xy", others + [(j, i) for i, j in others])
 
     send_list, rad = call(
         blend_body,
@@ -483,7 +489,7 @@
         [VMEM] * 8,
         [sds(potential_temp.shape, F32), sds((slots, slots), BF16), sds((slots, 128), F32)],
         (
-            potential_temp, wind_field, eddy_diff, district[:, owned + 16 : owned + 32, :], before, after,
+            potential_temp, wind_field, eddy_diff, district[:, owned + 16 : owned + 32, :], near, far,
             tile_send, speed,
         ),
     )
@@ -524,6 +530,4 @@
         P("xy", None, "gz"),
     )
     out_specs = (P("gz", "xy", None), P("gz", "xy", None, None))
-    return jax.shard_map(
-        on_device, mesh=mesh, in_specs=in_specs, out_specs=out_specs, check_vma=False
-    )
+    return jax.shard_map(on_device, mesh=mesh, in_specs=in_specs, out_specs=out_specs, check_vma=False)

time: 63.7 us -> 63.4 us (level)
  no operation moved by 1% of the time
where the time goes in v4:
time: 63.4 us; the launch traced here: 62.9 us
  starting transfers between devices  29.8 us (47%)
  Pallas kernels  11.5 us (18%)
  waiting for transfers between devices  10.4 us (16%)
  blocking collectives  9.68 us (15%)
  between operations  0.85 us (1%)
  local copies, waits for them, and re-layouts  0.69 us (1%)
    all_to_all x1, starting transfers between devices, on_device(): lax.all_to_all(send_list, 'xy', split_axis=0, concat_axis=0, tiled=True)  13.3 us
    pallas_call x7, Pallas kernels, call(): pl.pallas_call(body, in_specs=in_specs, out_specs=out_specs or tuple((VME...  11.5 us
    all_to_all x1, starting transfers between devices, on_device(): lax.all_to_all(payload, 'gz', split_axis=0, concat_axis=0, tiled=True)  11 us
    all_to_all x1, blocking collectives, on_device(): lax.all_to_all(contrib, 'gz', split_axis=0, concat_axis=0, tiled=True)  9.68 us
    all_to_all x1, waiting for transfers between devices, on_device(): lax.all_to_all(payload, 'gz', split_axis=0, concat_axis=0, tiled=True)  4.09 us
    all_to_all x1, waiting for transfers between devices, on_device(): lax.all_to_all(send_list, 'xy', split_axis=0, concat_axis=0, tiled=True)  3.77 us
    ppermute x1, starting transfers between devices, on_device(): lax.ppermute(jnp.where(even, first_row, last_row), 'xy', others + [(j, i)...  3.54 us
    ppermute x1, waiting for transfers between devices, on_device(): lax.ppermute(jnp.where(even, first_row, last_row), 'xy', others + [(j, i)...  2.57 us
  transfers between devices with their start and end apart: 4, of which 3 were waited for; matrix products, arithmetic and copies ran while one was open for 0% of the time, Pallas kernels for 7%

profile of v4, /device:TPU:1, one launch (start us, length us, event | category | flops | bytes accessed | tf_op | source)
XLA Modules:
  0.0 62.9 jit_solution(14951414851458263995)
XLA Ops:
  0.6 1.6 %shard_map.123 = bf16[8,96,128]{2,1,0:T(8,128)(2,1)} custom-call(f32[1,64,32,128]{3,2,1,0:T(8,128)} %wall_ref.3, s32[1,2,16]{2,1,0:T(2,128)} %pair_ref.3, f32[2,4,512]{2,1,0:T(4,128)} %theta_ref.5), custom_call_target="tpu_custom_call" | custom-call | bytes 1048576 | tf_op jit(solution)/shard_map/pallas_call | solution.py:27
  2.3 0.0 copy-start.3
  2.3 0.0 copy-start.7
  2.3 0.0 copy-start.9
  2.3 11.0 %all-to-all-start = ((bf16[8,96,128]{2,1,0:T(8,128)(2,1)}), bf16[8,96,128]{2,1,0:T(8,128)(2,1)S(1)}, u32[]{:S(2)}, u32[]{:S(2)}) async-start(bf16[8,96,128]{2,1,0:T(8,128)(2,1)} %shard_map.123), calls=%async_computation | async-start | bytes 393216 | tf_op jit(solution)/shard_map/all_to_all | solution.py:427
  13.3 0.0 copy-start.2
  13.3 0.0 copy-start.4
  13.3 0.0 copy-start.5
  13.4 2.7 %shard_map.124 = (f32[64,32,128]{2,1,0:T(8,128)S(1)}, f32[5,64,128]{2,1,0:T(8,128)S(1)}, f32[4,64,128]{2,1,0:T(8,128)S(1)}, f32[4,4,32,128]{3,2,1,0:T(8,128)S(1)...) custom-call(s32[1,64]{1,0:T(1,128)S(1)} %copy-done.7, ...), custom_call_target="tpu_custom_call" | custom-call | flops 75497472 | bytes 1048576 | tf_op jit(solution)/shard_map/pallas_call | solution.py:27
  16.1 0.0 copy-start.10
  16.1 0.6 copy-done.8
  16.8 1.4 %shard_map.122 = (f32[128,128]{1,0:T(8,128)S(1)}, f32[128,128]{1,0:T(8,128)S(1)}, f32[4,64,128]{2,1,0:T(8,128)S(1)}, s32[1,2,16]{2,1,0:T(2,128)S(1)}) custom-call(f32[2,4,512]{2,1,0:T(4,128)S(1)} %copy-done.2, f32[3,2,4,512]{3,2,1,0:T(4,128)S(1)} %copy-done.5, s32[128,128]{1,0:T(8,128)S(1)} %bitcast.4, s32[1,128]{1,0:T(1,128)S(1)} %copy-done.10, ...), custom_call_target="tpu_custom_call" | custom-call | flops 402653184 | bytes 1048576 | tf_op jit(solution)/shard_map/pallas_call | solution.py:27
  18.2 4.1 %all-to-all-done.recv_ref = bf16[8,96,128]{2,1,0:T(8,128)(2,1)S(1)} async-done(((bf16[8,96,128]{2,1,0:T(8,128)(2,1)}), bf16[8,96,128]{2,1,0:T(8,128)(2,1)S(1)}, u32[]{:S(2)}, u32[]{:S(2)}) %all-to-all-start) | async-done | bytes 196640 | tf_op jit(solution)/shard_map/all_to_all | solution.py:427
  22.3 0.9 %shard_map.125 = (bf16[8,16,128]{2,1,0:T(8,128)(2,1)S(1)}, bf16[64,128]{1,0:T(8,128)(2,1)S(1)}) custom-call(s32[1,2,16]{2,1,0:T(2,128)S(1)} %get-tuple-element.28.pair_ref, bf16[8,96,128]{2,1,0:T(8,128)(2,1)S(1)} %all-to-all-done.recv_ref, bf16[1,16,128,128]{3,2,1,0:T(8,128)(2,1)S(1)} %copy-done.1), custom_call_target="tpu_custom_call" | custom-call | bytes 1048576 | tf_op jit(solution)/shard_map/pallas_call | solution.py:27
  23.2 9.7 %all_to_all.21.refl_ref = bf16[8,16,128]{2,1,0:T(8,128)(2,1)S(1)} all-to-all(bf16[8,16,128]{2,1,0:T(8,128)(2,1)S(1)} %get-tuple-element.32), channel_id=1, replica_groups=mesh['xy'=64,'gz'=8] {'gz'}, dimensions={0} | all-to-all | bytes 65536 | tf_op jit(solution)/shard_map/all_to_all | solution.py:470
  32.9 1.1 %shard_map.126 = (bf16[1024,128]{1,0:T(8,128)(2,1)}, f32[64,128]{1,0:T(8,128)S(1)}) custom-call(bf16[8,16,128]{2,1,0:T(8,128)(2,1)S(1)} %all_to_all.21.refl_ref, bf16[64,128]{1,0:T(8,128)(2,1)S(1)} %get-tuple-element.33.add_ref, f32[5,64,128]{2,1,0:T(8,128)S(1)} %get-tuple-element.34.rows_ref, f32[4,64,128]{2,1,0:T(8,128)S(1)} %get-tuple-element.35.lam_ref, ...), custom_call_target="tpu_custom_call" | custom-call | bytes 1048576 | tf_op jit(solution)/shard_map/pallas_call | solution.py:27
  34.0 13.3 %all-to-all-start.2 = ((bf16[64,16,128]{2,1,0:T(8,128)(2,1)}), bf16[64,16,128]{2,1,0:T(8,128)(2,1)S(1)}, u32[]{:S(2)}, u32[]{:S(2)}) async-start(bf16[64,16,128]{2,1,0:T(8,128)(2,1)} %bitcast.1), calls=%async_computation.2 | async-start | bytes 524288 | tf_op jit(solution)/shard_map/all_to_all | solution.py:486
  47.3 3.5 %collective-permute-start.1 = (f32[2,1,512]{2,1,0:T(1,128)S(1)}, f32[2,1,512]{2,1,0:T(1,128)S(1)}, u32[]{:S(2)}, u32[]{:S(2)}) collective-permute-start(f32[2,1,512]{2,1,0:T(1,128)S(1)} %get-tuple-element.54), channel_id=1, source_target_pairs={{8,16},{24,32},{40,48},{56,64},{72,80},{88,96},{104,112},{120,128}... | collective-permute-start | bytes 12296 | tf_op jit(solution)/shard_map/ppermute | solution.py:477
  50.9 0.0 copy-start.6
  50.9 1.9 %collective-permute-start = (f32[2,1,512]{2,1,0:T(1,128)S(1)}, f32[2,1,512]{2,1,0:T(1,128)S(1)}, u32[]{:S(2)}, u32[]{:S(2)}) collective-permute-start(f32[2,1,512]{2,1,0:T(1,128)S(1)} %get-tuple-element.55), channel_id=1, source_target_pairs={{0,8},{16,24},{32,40},{48,56},{64,72},{80,88},{96,104},{112,120},{... | collective-permute-start | bytes 12296 | tf_op jit(solution)/shard_map/ppermute | solution.py:476
  52.8 2.6 %collective-permute-done.1.far_ref = f32[2,1,512]{2,1,0:T(1,128)S(1)} collective-permute-done((f32[2,1,512]{2,1,0:T(1,128)S(1)}, f32[2,1,512]{2,1,0:T(1,128)S(1)}, u32[]{:S(2)}, u32[]{:S(2)}) %collective-permute-start.1) | collective-permute-done | bytes 4128 | tf_op jit(solution)/shard_map/ppermute | solution.py:477
  55.4 0.1 shard_map.127
  55.5 3.8 %all-to-all-done.2 = bf16[64,16,128]{2,1,0:T(8,128)(2,1)S(1)} async-done(((bf16[64,16,128]{2,1,0:T(8,128)(2,1)}), bf16[64,16,128]{2,1,0:T(8,128)(2,1)S(1)}, u32[]{:S(2)}, u32[]{:S(2)}) %all-to-all-start.2) | async-done | bytes 262176 | tf_op jit(solution)/shard_map/all_to_all | solution.py:486
  59.3 3.6 %shard_map.128 = (f32[1,64,32,128]{3,2,1,0:T(8,128)}, f32[2,4,512]{2,1,0:T(4,128)}) custom-call(s32[1,64]{1,0:T(1,128)S(1)} %copy-done.7, bf16[1024,128]{1,0:T(8,128)(2,1)S(1)} %bitcast.3, bf16[64,128]{1,0:T(8,128)(2,1)S(1)} %get-tuple-element.41.take_ref, f32[5,64,128]{2,1,0:T(8,128)S(1)} %get-tuple-element.34.rows_ref, ...), custom_call_target="tpu_custom_call" | custom-call | flops 268435456 | bytes 1048576 | tf_op jit(solution)/shard_map/pallas_call | solution.py:27
  (16 shorter events, 0.0 us)
Async XLA Ops:
  0.6 12.7 %copy-start = (f32[1,64,32,128]{3,2,1,0:T(8,128)S(1)}, f32[1,64,32,128]{3,2,1,0:T(8,128)}, u32[]{:S(2)}) copy-start(f32[1,64,32,128]{3,2,1,0:T(8,128)} %wall_ref.3) | copy-start | bytes 3145732
  2.3 11.0 %copy-start.3 = (f32[4,32,32]{2,1,0:T(8,128)S(1)}, f32[4,32,32]{2,1,0:T(8,128)}, u32[]{:S(2)}) copy-start(f32[4,32,32]{2,1,0:T(8,128)} %inverse_ref.1) | copy-start | bytes 49156
  2.3 11.0 %copy-start.7 = (s32[1,64]{1,0:T(1,128)S(1)}, s32[1,64]{1,0:T(1,128)}, u32[]{:S(2)}) copy-start(s32[1,64]{1,0:T(1,128)} %class_ref.3) | copy-start | bytes 772
  2.3 11.0 %copy-start.9 = (s32[1,64]{1,0:T(1,128)S(1)}, s32[1,64]{1,0:T(1,128)}, u32[]{:S(2)}) copy-start(s32[1,64]{1,0:T(1,128)} %take_ref.1) | copy-start | bytes 772
  2.3 20.0 %all-to-all-start = ((bf16[8,96,128]{2,1,0:T(8,128)(2,1)}), bf16[8,96,128]{2,1,0:T(8,128)(2,1)S(1)}, u32[]{:S(2)}, u32[]{:S(2)}) async-start(bf16[8,96,128]{2,1,0:T(8,128)(2,1)} %shard_map.123), calls=%async_computation | async-start | bytes 393216 | tf_op jit(solution)/shard_map/all_to_all | solution.py:427
  13.3 2.8 %copy-start.2 = (f32[2,4,512]{2,1,0:T(4,128)S(1)}, f32[2,4,512]{2,1,0:T(4,128)}, u32[]{:S(2)}) copy-start(f32[2,4,512]{2,1,0:T(4,128)} %theta_ref.5) | copy-start | bytes 49156
  13.3 2.8 %copy-start.4 = (s32[1,128,128]{2,1,0:T(8,128)S(1)}, s32[1,128,128]{2,1,0:T(8,128)}, u32[]{:S(2)}) copy-start(s32[1,128,128]{2,1,0:T(8,128)} %param.14) | copy-start | bytes 196612
  13.3 2.8 %copy-start.5 = (f32[3,2,4,512]{3,2,1,0:T(4,128)S(1)}, f32[3,2,4,512]{3,2,1,0:T(4,128)}, u32[]{:S(2)}) copy-start(f32[3,2,4,512]{3,2,1,0:T(4,128)} %wind_ref.3) | copy-start | bytes 147460
  16.1 0.7 %copy-start.8 = (s32[1,2,16]{2,1,0:T(2,128)S(1)}, s32[1,2,16]{2,1,0:T(2,128)}, u32[]{:S(2)}) copy-start(s32[1,2,16]{2,1,0:T(2,128)} %pair_ref.3) | copy-start | bytes 388
  16.1 0.7 %copy-start.10 = (s32[1,128]{1,0:T(1,128)S(1)}, s32[1,128]{1,0:T(1,128)}, u32[]{:S(2)}) copy-start(s32[1,128]{1,0:T(1,128)} %send_ref.3) | copy-start | bytes 1540
  16.8 5.5 %copy-start.1 = (bf16[1,16,128,128]{3,2,1,0:T(8,128)(2,1)S(1)}, bf16[1,16,128,128]{3,2,1,0:T(8,128)(2,1)}, u32[]{:S(2)}) copy-start(bf16[1,16,128,128]{3,2,1,0:T(8,128)(2,1)} %block_ref.1) | copy-start | bytes 1572868
  34.0 25.3 %all-to-all-start.2 = ((bf16[64,16,128]{2,1,0:T(8,128)(2,1)}), bf16[64,16,128]{2,1,0:T(8,128)(2,1)S(1)}, u32[]{:S(2)}, u32[]{:S(2)}) async-start(bf16[64,16,128]{2,1,0:T(8,128)(2,1)} %bitcast.1), calls=%async_computation.2 | async-start | bytes 524288 | tf_op jit(solution)/shard_map/all_to_all | solution.py:486
  47.3 8.1 %collective-permute-start.1 = (f32[2,1,512]{2,1,0:T(1,128)S(1)}, f32[2,1,512]{2,1,0:T(1,128)S(1)}, u32[]{:S(2)}, u32[]{:S(2)}) collective-permute-start(f32[2,1,512]{2,1,0:T(1,128)S(1)} %get-tuple-element.54), channel_id=1, source_target_pairs={{8,16},{24,32},{40,48},{56,64},{72,80},{88,96},{104,112},{120,128}... | collective-permute-start | bytes 12296 | tf_op jit(solution)/shard_map/ppermute | solution.py:477
  50.9 4.5 %copy-start.6 = (f32[2,4,512]{2,1,0:T(4,128)S(1)}, f32[2,4,512]{2,1,0:T(4,128)}, u32[]{:S(2)}) copy-start(f32[2,4,512]{2,1,0:T(4,128)} %eddy_ref.1) | copy-start | bytes 49156
  50.9 4.5 %collective-permute-start = (f32[2,1,512]{2,1,0:T(1,128)S(1)}, f32[2,1,512]{2,1,0:T(1,128)S(1)}, u32[]{:S(2)}, u32[]{:S(2)}) collective-permute-start(f32[2,1,512]{2,1,0:T(1,128)S(1)} %get-tuple-element.55), channel_id=1, source_target_pairs={{0,8},{16,24},{32,40},{48,56},{64,72},{80,88},{96,104},{112,120},{... | collective-permute-start | bytes 12296 | tf_op jit(solution)/shard_map/ppermute | solution.py:476

commit v5 on v4

--- a/solution.py
+++ b/solution.py
@@ -80,8 +80,8 @@
         up = jnp.where(level + 1 == dest, plane_ref[1], 0.0)
         down = jnp.where(level - 1 == dest, plane_ref[0], 0.0)
         out_ref[dest, 0:owned, :] = emitted
-        out_ref[dest, owned : owned + 16, :] = ids_ref[...].astype(BF16)
-        out_ref[dest, owned + 16 : owned + 32, :] = (up + down).astype(BF16)
+        out_ref[dest, owned : owned + 8, :] = ids_ref[...].astype(BF16)
+        out_ref[dest, owned + 8 : owned + 24, :] = (up + down).astype(BF16)
 
 
 def lookup_body(
@@ -136,7 +136,7 @@
     ids = jnp.zeros((1, 128), F32)
     for part in range(parts):
         all_ref[part * owned : (part + 1) * owned, :] = recv_ref[part, 0:owned, :].astype(F32)
-        row = recv_ref[part, owned : owned + 16, :].astype(F32)[0:1, :]
+        row = recv_ref[part, owned : owned + 8, :].astype(F32)[0:1, :]
         row = jnp.where(lane < blocks, row, 0.0)
         ids = ids + (pltpu.roll(row, part * blocks, 1) if part else row)
     for b in range(blocks):
@@ -412,13 +412,13 @@
     (payload,) = call(
         pack_body,
         [HBM] * 3,
-        [sds((parts, owned + 32, 128), BF16)],
+        [sds((parts, owned + 24, 128), BF16)],
         (wall_temp, refl_pair, potential_temp),
         [
             pltpu.VMEM((owned, 128), F32),
             pltpu.VMEM(refl_pair.shape, jnp.int32),
             pltpu.VMEM(potential_temp.shape, F32),
-            pltpu.VMEM((16, 128), F32),
+            pltpu.VMEM((8, 128), F32),
             pltpu.VMEM((2, 16, 128), F32),
             dma((3,)),
         ],
@@ -489,7 +489,7 @@
         [VMEM] * 8,
         [sds(potential_temp.shape, F32), sds((slots, slots), BF16), sds((slots, 128), F32)],
         (
-            potential_temp, wind_field, eddy_diff, district[:, owned + 16 : owned + 32, :], near, far,
+            potential_temp, wind_field, eddy_diff, district[:, owned + 8 : owned + 24, :], near, far,
             tile_send, speed,
         ),
     )

time: 63.4 us -> 63 us (level)
  no operation moved by 1% of the time
where the time goes in v5:
time: 63 us; the launch traced here: 62.6 us
  starting transfers between devices  29.8 us (47%)
  Pallas kernels  11.5 us (18%)
  waiting for transfers between devices  10.1 us (16%)
  blocking collectives  9.62 us (15%)
  between operations  0.85 us (1%)
  local copies, waits for them, and re-layouts  0.69 us (1%)
    all_to_all x1, starting transfers between devices, on_device(): lax.all_to_all(send_list, 'xy', split_axis=0, concat_axis=0, tiled=True)  13.4 us
    pallas_call x7, Pallas kernels, call(): pl.pallas_call(body, in_specs=in_specs, out_specs=out_specs or tuple((VME...  11.5 us
    all_to_all x1, starting transfers between devices, on_device(): lax.all_to_all(payload, 'gz', split_axis=0, concat_axis=0, tiled=True)  11 us
    all_to_all x1, blocking collectives, on_device(): lax.all_to_all(contrib, 'gz', split_axis=0, concat_axis=0, tiled=True)  9.62 us
    all_to_all x1, waiting for transfers between devices, on_device(): lax.all_to_all(send_list, 'xy', split_axis=0, concat_axis=0, tiled=True)  3.77 us
    all_to_all x1, waiting for transfers between devices, on_device(): lax.all_to_all(payload, 'gz', split_axis=0, concat_axis=0, tiled=True)  3.76 us
    ppermute x1, starting transfers between devices, on_device(): lax.ppermute(jnp.where(even, first_row, last_row), 'xy', others + [(j, i)...  3.54 us
    ppermute x1, waiting for transfers between devices, on_device(): lax.ppermute(jnp.where(even, first_row, last_row), 'xy', others + [(j, i)...  2.57 us
  transfers between devices with their start and end apart: 4, of which 3 were waited for; matrix products, arithmetic and copies ran while one was open for 0% of the time, Pallas kernels for 7%

profile of v5, /device:TPU:1, one launch (start us, length us, event | category | flops | bytes accessed | tf_op | source)
XLA Modules:
  0.0 62.6 jit_solution(7546536640506841194)
XLA Ops:
  0.6 1.6 %shard_map.123 = bf16[8,88,128]{2,1,0:T(8,128)(2,1)} custom-call(f32[1,64,32,128]{3,2,1,0:T(8,128)} %wall_ref.3, s32[1,2,16]{2,1,0:T(2,128)} %pair_ref.3, f32[2,4,512]{2,1,0:T(4,128)} %theta_ref.5), custom_call_target="tpu_custom_call" | custom-call | bytes 1048576 | tf_op jit(solution)/shard_map/pallas_call | solution.py:27
  2.2 0.0 copy-start.3
  2.3 0.0 copy-start.7
  2.3 0.0 copy-start.9
  2.3 11.0 %all-to-all-start = ((bf16[8,88,128]{2,1,0:T(8,128)(2,1)}), bf16[8,88,128]{2,1,0:T(8,128)(2,1)S(1)}, u32[]{:S(2)}, u32[]{:S(2)}) async-start(bf16[8,88,128]{2,1,0:T(8,128)(2,1)} %shard_map.123), calls=%async_computation | async-start | bytes 360448 | tf_op jit(solution)/shard_map/all_to_all | solution.py:427
  13.3 0.0 copy-start.2
  13.3 0.0 copy-start.4
  13.3 0.0 copy-start.5
  13.4 2.7 %shard_map.124 = (f32[64,32,128]{2,1,0:T(8,128)S(1)}, f32[5,64,128]{2,1,0:T(8,128)S(1)}, f32[4,64,128]{2,1,0:T(8,128)S(1)}, f32[4,4,32,128]{3,2,1,0:T(8,128)S(1)...) custom-call(s32[1,64]{1,0:T(1,128)S(1)} %copy-done.7, ...), custom_call_target="tpu_custom_call" | custom-call | flops 75497472 | bytes 1048576 | tf_op jit(solution)/shard_map/pallas_call | solution.py:27
  16.1 0.0 copy-start.8
  16.1 0.0 copy-start.10
  16.1 0.6 %copy-done.8 = s32[1,2,16]{2,1,0:T(2,128)S(1)} copy-done((s32[1,2,16]{2,1,0:T(2,128)S(1)}, s32[1,2,16]{2,1,0:T(2,128)}, u32[]{:S(2)}) %copy-start.8) | copy-done | bytes 152
  16.7 1.4 %shard_map.122 = (f32[128,128]{1,0:T(8,128)S(1)}, f32[128,128]{1,0:T(8,128)S(1)}, f32[4,64,128]{2,1,0:T(8,128)S(1)}, s32[1,2,16]{2,1,0:T(2,128)S(1)}) custom-call(f32[2,4,512]{2,1,0:T(4,128)S(1)} %copy-done.2, f32[3,2,4,512]{3,2,1,0:T(4,128)S(1)} %copy-done.5, s32[128,128]{1,0:T(8,128)S(1)} %bitcast.4, s32[1,128]{1,0:T(1,128)S(1)} %copy-done.10, ...), custom_call_target="tpu_custom_call" | custom-call | flops 402653184 | bytes 1048576 | tf_op jit(solution)/shard_map/pallas_call | solution.py:27
  18.2 3.8 %all-to-all-done.recv_ref = bf16[8,88,128]{2,1,0:T(8,128)(2,1)S(1)} async-done(((bf16[8,88,128]{2,1,0:T(8,128)(2,1)}), bf16[8,88,128]{2,1,0:T(8,128)(2,1)S(1)}, u32[]{:S(2)}, u32[]{:S(2)}) %all-to-all-start) | async-done | bytes 180256 | tf_op jit(solution)/shard_map/all_to_all | solution.py:427
  21.9 0.9 %shard_map.125 = (bf16[8,16,128]{2,1,0:T(8,128)(2,1)S(1)}, bf16[64,128]{1,0:T(8,128)(2,1)S(1)}) custom-call(s32[1,2,16]{2,1,0:T(2,128)S(1)} %get-tuple-element.28.pair_ref, bf16[8,88,128]{2,1,0:T(8,128)(2,1)S(1)} %all-to-all-done.recv_ref, bf16[1,16,128,128]{3,2,1,0:T(8,128)(2,1)S(1)} %copy-done.1), custom_call_target="tpu_custom_call" | custom-call | bytes 1048576 | tf_op jit(solution)/shard_map/pallas_call | solution.py:27
  22.8 9.6 %all_to_all.21.refl_ref = bf16[8,16,128]{2,1,0:T(8,128)(2,1)S(1)} all-to-all(bf16[8,16,128]{2,1,0:T(8,128)(2,1)S(1)} %get-tuple-element.32), channel_id=1, replica_groups=mesh['xy'=64,'gz'=8] {'gz'}, dimensions={0} | all-to-all | bytes 65536 | tf_op jit(solution)/shard_map/all_to_all | solution.py:470
  32.4 1.1 %shard_map.126 = (bf16[1024,128]{1,0:T(8,128)(2,1)}, f32[64,128]{1,0:T(8,128)S(1)}) custom-call(bf16[8,16,128]{2,1,0:T(8,128)(2,1)S(1)} %all_to_all.21.refl_ref, bf16[64,128]{1,0:T(8,128)(2,1)S(1)} %get-tuple-element.33.add_ref, f32[5,64,128]{2,1,0:T(8,128)S(1)} %get-tuple-element.34.rows_ref, f32[4,64,128]{2,1,0:T(8,128)S(1)} %get-tuple-element.35.lam_ref, ...), custom_call_target="tpu_custom_call" | custom-call | bytes 1048576 | tf_op jit(solution)/shard_map/pallas_call | solution.py:27
  33.5 13.4 %all-to-all-start.2 = ((bf16[64,16,128]{2,1,0:T(8,128)(2,1)}), bf16[64,16,128]{2,1,0:T(8,128)(2,1)S(1)}, u32[]{:S(2)}, u32[]{:S(2)}) async-start(bf16[64,16,128]{2,1,0:T(8,128)(2,1)} %bitcast.1), calls=%async_computation.2 | async-start | bytes 524288 | tf_op jit(solution)/shard_map/all_to_all | solution.py:486
  47.0 3.5 %collective-permute-start.1 = (f32[2,1,512]{2,1,0:T(1,128)S(1)}, f32[2,1,512]{2,1,0:T(1,128)S(1)}, u32[]{:S(2)}, u32[]{:S(2)}) collective-permute-start(f32[2,1,512]{2,1,0:T(1,128)S(1)} %get-tuple-element.54), channel_id=1, source_target_pairs={{8,16},{24,32},{40,48},{56,64},{72,80},{88,96},{104,112},{120,128}... | collective-permute-start | bytes 12296 | tf_op jit(solution)/shard_map/ppermute | solution.py:477
  50.5 1.9 %collective-permute-start = (f32[2,1,512]{2,1,0:T(1,128)S(1)}, f32[2,1,512]{2,1,0:T(1,128)S(1)}, u32[]{:S(2)}, u32[]{:S(2)}) collective-permute-start(f32[2,1,512]{2,1,0:T(1,128)S(1)} %get-tuple-element.55), channel_id=1, source_target_pairs={{0,8},{16,24},{32,40},{48,56},{64,72},{80,88},{96,104},{112,120},{... | collective-permute-start | bytes 12296 | tf_op jit(solution)/shard_map/ppermute | solution.py:476
  52.5 2.6 %collective-permute-done.1.far_ref = f32[2,1,512]{2,1,0:T(1,128)S(1)} collective-permute-done((f32[2,1,512]{2,1,0:T(1,128)S(1)}, f32[2,1,512]{2,1,0:T(1,128)S(1)}, u32[]{:S(2)}, u32[]{:S(2)}) %collective-permute-start.1) | collective-permute-done | bytes 4128 | tf_op jit(solution)/shard_map/ppermute | solution.py:477
  55.0 0.1 shard_map.127
  55.2 3.8 %all-to-all-done.2 = bf16[64,16,128]{2,1,0:T(8,128)(2,1)S(1)} async-done(((bf16[64,16,128]{2,1,0:T(8,128)(2,1)}), bf16[64,16,128]{2,1,0:T(8,128)(2,1)S(1)}, u32[]{:S(2)}, u32[]{:S(2)}) %all-to-all-start.2) | async-done | bytes 262176 | tf_op jit(solution)/shard_map/all_to_all | solution.py:486
  58.9 3.6 %shard_map.128 = (f32[1,64,32,128]{3,2,1,0:T(8,128)}, f32[2,4,512]{2,1,0:T(4,128)}) custom-call(s32[1,64]{1,0:T(1,128)S(1)} %copy-done.7, bf16[1024,128]{1,0:T(8,128)(2,1)S(1)} %bitcast.3, bf16[64,128]{1,0:T(8,128)(2,1)S(1)} %get-tuple-element.41.take_ref, f32[5,64,128]{2,1,0:T(8,128)S(1)} %get-tuple-element.34.rows_ref, ...), custom_call_target="tpu_custom_call" | custom-call | flops 268435456 | bytes 1048576 | tf_op jit(solution)/shard_map/pallas_call | solution.py:27
  (16 shorter events, 0.0 us)
Async XLA Ops:
  0.6 12.7 %copy-start = (f32[1,64,32,128]{3,2,1,0:T(8,128)S(1)}, f32[1,64,32,128]{3,2,1,0:T(8,128)}, u32[]{:S(2)}) copy-start(f32[1,64,32,128]{3,2,1,0:T(8,128)} %wall_ref.3) | copy-start | bytes 3145732
  2.2 11.0 %copy-start.3 = (f32[4,32,32]{2,1,0:T(8,128)S(1)}, f32[4,32,32]{2,1,0:T(8,128)}, u32[]{:S(2)}) copy-start(f32[4,32,32]{2,1,0:T(8,128)} %inverse_ref.1) | copy-start | bytes 49156
  2.3 11.0 %copy-start.7 = (s32[1,64]{1,0:T(1,128)S(1)}, s32[1,64]{1,0:T(1,128)}, u32[]{:S(2)}) copy-start(s32[1,64]{1,0:T(1,128)} %class_ref.3) | copy-start | bytes 772
  2.3 11.0 %copy-start.9 = (s32[1,64]{1,0:T(1,128)S(1)}, s32[1,64]{1,0:T(1,128)}, u32[]{:S(2)}) copy-start(s32[1,64]{1,0:T(1,128)} %take_ref.1) | copy-start | bytes 772
  2.3 19.7 %all-to-all-start = ((bf16[8,88,128]{2,1,0:T(8,128)(2,1)}), bf16[8,88,128]{2,1,0:T(8,128)(2,1)S(1)}, u32[]{:S(2)}, u32[]{:S(2)}) async-start(bf16[8,88,128]{2,1,0:T(8,128)(2,1)} %shard_map.123), calls=%async_computation | async-start | bytes 360448 | tf_op jit(solution)/shard_map/all_to_all | solution.py:427
  13.3 2.8 %copy-start.2 = (f32[2,4,512]{2,1,0:T(4,128)S(1)}, f32[2,4,512]{2,1,0:T(4,128)}, u32[]{:S(2)}) copy-start(f32[2,4,512]{2,1,0:T(4,128)} %theta_ref.5) | copy-start | bytes 49156
  13.3 2.8 %copy-start.4 = (s32[1,128,128]{2,1,0:T(8,128)S(1)}, s32[1,128,128]{2,1,0:T(8,128)}, u32[]{:S(2)}) copy-start(s32[1,128,128]{2,1,0:T(8,128)} %param.14) | copy-start | bytes 196612
  13.3 2.8 %copy-start.5 = (f32[3,2,4,512]{3,2,1,0:T(4,128)S(1)}, f32[3,2,4,512]{3,2,1,0:T(4,128)}, u32[]{:S(2)}) copy-start(f32[3,2,4,512]{3,2,1,0:T(4,128)} %wind_ref.3) | copy-start | bytes 147460
  16.1 0.7 %copy-start.8 = (s32[1,2,16]{2,1,0:T(2,128)S(1)}, s32[1,2,16]{2,1,0:T(2,128)}, u32[]{:S(2)}) copy-start(s32[1,2,16]{2,1,0:T(2,128)} %pair_ref.3) | copy-start | bytes 388
  16.1 0.7 %copy-start.10 = (s32[1,128]{1,0:T(1,128)S(1)}, s32[1,128]{1,0:T(1,128)}, u32[]{:S(2)}) copy-start(s32[1,128]{1,0:T(1,128)} %send_ref.3) | copy-start | bytes 1540
  16.7 5.2 %copy-start.1 = (bf16[1,16,128,128]{3,2,1,0:T(8,128)(2,1)S(1)}, bf16[1,16,128,128]{3,2,1,0:T(8,128)(2,1)}, u32[]{:S(2)}) copy-start(bf16[1,16,128,128]{3,2,1,0:T(8,128)(2,1)} %block_ref.1) | copy-start | bytes 1572868
  33.5 25.4 %all-to-all-start.2 = ((bf16[64,16,128]{2,1,0:T(8,128)(2,1)}), bf16[64,16,128]{2,1,0:T(8,128)(2,1)S(1)}, u32[]{:S(2)}, u32[]{:S(2)}) async-start(bf16[64,16,128]{2,1,0:T(8,128)(2,1)} %bitcast.1), calls=%async_computation.2 | async-start | bytes 524288 | tf_op jit(solution)/shard_map/all_to_all | solution.py:486
  47.0 8.1 %collective-permute-start.1 = (f32[2,1,512]{2,1,0:T(1,128)S(1)}, f32[2,1,512]{2,1,0:T(1,128)S(1)}, u32[]{:S(2)}, u32[]{:S(2)}) collective-permute-start(f32[2,1,512]{2,1,0:T(1,128)S(1)} %get-tuple-element.54), channel_id=1, source_target_pairs={{8,16},{24,32},{40,48},{56,64},{72,80},{88,96},{104,112},{120,128}... | collective-permute-start | bytes 12296 | tf_op jit(solution)/shard_map/ppermute | solution.py:477
  50.5 4.5 %copy-start.6 = (f32[2,4,512]{2,1,0:T(4,128)S(1)}, f32[2,4,512]{2,1,0:T(4,128)}, u32[]{:S(2)}) copy-start(f32[2,4,512]{2,1,0:T(4,128)} %eddy_ref.1) | copy-start | bytes 49156
  50.5 4.5 %collective-permute-start = (f32[2,1,512]{2,1,0:T(1,128)S(1)}, f32[2,1,512]{2,1,0:T(1,128)S(1)}, u32[]{:S(2)}, u32[]{:S(2)}) collective-permute-start(f32[2,1,512]{2,1,0:T(1,128)S(1)} %get-tuple-element.55), channel_id=1, source_target_pairs={{0,8},{16,24},{32,40},{48,56},{64,72},{80,88},{96,104},{112,120},{... | collective-permute-start | bytes 12296 | tf_op jit(solution)/shard_map/ppermute | solution.py:476
